TPU v7x, 1024 devices: a whole 4x4x32 slice. The times are simulated.
1024 devices in a mesh: section: 4 (over y), hid: 32 (over z), wid: 8 (over x, core).
Axes of the slice: x: 4, y: 4, z: 32, core: 2. Of those that a mesh axis runs over, the one named last changes fastest.
Arguments:
- out_grad: bfloat16 [512, 8192], P(('section', 'hid'), 'wid'), may hold values from -6 to 6
- inputs: bfloat16 [512, 8192], P(('section', 'hid'), 'wid'), may hold values from -6 to 6
- gate_pre: bfloat16 [512, 14336], P(('section', 'wid'), 'hid'), may hold values from -6 to 6
- up_pre: bfloat16 [512, 14336], P(('section', 'wid'), 'hid'), may hold values from -6 to 6
- w1_values: bfloat16 [40960, 4096], P(('section', 'hid', 'wid')), may hold values from -0.09375 to 0.09375
- w1_index: int32 [40960], P(('section', 'hid', 'wid')), may hold values from 0 to 112, as said below
- w3_values: bfloat16 [40960, 4096], P(('section', 'hid', 'wid')), may hold values from -0.09375 to 0.09375
- w3_index: int32 [40960], P(('section', 'hid', 'wid')), may hold values from 0 to 112, as said below
- w2_values: bfloat16 [40960, 4096], P(('section', 'hid', 'wid')), may hold values from -0.125 to 0.125
- w2_index: int32 [40960], P(('section', 'hid', 'wid')), may hold values from 0 to 112, as said below
Outputs:
- input_grad: bfloat16 [512, 8192], P(('section', 'hid'), 'wid')
- w1_grad: bfloat16 [40960, 4096], P(('section', 'hid', 'wid'))
- w3_grad: bfloat16 [40960, 4096], P(('section', 'hid', 'wid'))
- w2_grad: bfloat16 [40960, 4096], P(('section', 'hid', 'wid'))
Inputs may be any that keep to these rules, and one draw needn't show every extreme that they name: `w1_index`: on each device, its 40 slots hold distinct block numbers of its tile first, then the tile's block count in every unused slot; the number of used slots differs from device to device, and some device of every matrix uses all 40. `w3_index`: as for w1_index. `w2_index`: as for w1_index.
All inputs are finite; a program needn't handle non-finite values.
Results may differ from a plain program's by a relative error of at most 0.0049.
Values may be sent and summed in bfloat16 or wider, within the bound.
No kernel may reach another device: no remote copies, remote signals or barrier semaphores. Data moves between devices by JAX's collectives and lax.ppermute only.
A program may use at most 32 MiB of HBM per device.

v0:
```python
import jax
import jax.numpy as jnp
from jax import lax
from jax.sharding import PartitionSpec as P

BLOCK = 64


def from_behind(shard, axis, by):
    peers = lax.axis_size(axis)
    return lax.ppermute(shard, axis, [(i, (i + by) % peers) for i in range(peers)])


def dense_local(values, index, rows, cols):
    blocks = values.reshape(values.shape[0], BLOCK, BLOCK)
    total = rows * cols
    holder = jnp.zeros((total + 1, BLOCK, BLOCK), values.dtype).at[index].set(blocks)
    return (
        holder[:total]
        .reshape(rows, cols, BLOCK, BLOCK)
        .transpose(0, 2, 1, 3)
        .reshape(rows * BLOCK, cols * BLOCK)
    )


def slots_from(dense, index, rows, cols):
    blocks = (
        dense.reshape(rows, BLOCK, cols, BLOCK)
        .transpose(0, 2, 1, 3)
        .reshape(rows * cols, BLOCK, BLOCK)
    )
    blocks = jnp.concatenate([blocks, jnp.zeros((1, BLOCK, BLOCK), dense.dtype)], axis=0)
    return blocks[index].reshape(index.shape[0], BLOCK * BLOCK)


def swiglu_grads(hidden_grad, gate_pre, up_pre):
    gate = gate_pre.astype(jnp.float32)
    upval = up_pre.astype(jnp.float32)
    sigma = jax.nn.sigmoid(gate)
    gate_grad = (hidden_grad * upval * sigma * (1.0 + gate * (1.0 - sigma))).astype(jnp.bfloat16)
    up_grad = (hidden_grad * gate * sigma).astype(jnp.bfloat16)
    activ = (gate * sigma * upval).astype(jnp.bfloat16)
    return (gate_grad, up_grad, activ)


def body(
    out_grad,
    inputs,
    gate_pre,
    up_pre,
    w1_values,
    w1_index,
    w3_values,
    w3_index,
    w2_values,
    w2_index,
):
    arrived = from_behind(out_grad, "section", -1)
    grad_all, input_all = (
        lax.all_gather(arrived, "hid", axis=0, tiled=True),
        lax.all_gather(inputs, "hid", axis=0, tiled=True),
    )
    rows = inputs.shape[1] // BLOCK
    cols = gate_pre.shape[1] // BLOCK
    first = dense_local(w1_values, w1_index, rows, cols)
    third = dense_local(w3_values, w3_index, rows, cols)
    second = dense_local(w2_values, w2_index, cols, rows)
    partial_grad = jnp.einsum("td,fd->tf", grad_all, second, preferred_element_type=jnp.float32)
    hidden_grad = lax.psum(partial_grad, "wid")
    gate_all, up_all = (
        lax.all_gather(gate_pre, "wid", axis=0, tiled=True),
        lax.all_gather(up_pre, "wid", axis=0, tiled=True),
    )
    gate_grad, up_grad, activ = swiglu_grads(hidden_grad, gate_all, up_all)
    own_rows = inputs.shape[0]
    total = jnp.einsum("tf,df->td", gate_grad, first, preferred_element_type=jnp.float32)
    summed = lax.psum(
        total + jnp.einsum("tf,df->td", up_grad, third, preferred_element_type=jnp.float32), "hid"
    )
    offset = lax.axis_index("hid") * own_rows
    input_grad = lax.dynamic_slice_in_dim(summed, offset, own_rows, 0).astype(jnp.bfloat16)
    first_grad = jnp.einsum(
        "td,tf->df", input_all, gate_grad, preferred_element_type=jnp.float32
    ).astype(jnp.bfloat16)
    third_grad = jnp.einsum(
        "td,tf->df", input_all, up_grad, preferred_element_type=jnp.float32
    ).astype(jnp.bfloat16)
    second_grad = jnp.einsum(
        "tf,td->fd", activ, grad_all, preferred_element_type=jnp.float32
    ).astype(jnp.bfloat16)
    w1_grad = slots_from(first_grad, w1_index, rows, cols)
    w3_grad = slots_from(third_grad, w3_index, rows, cols)
    w2_grad = slots_from(second_grad, w2_index, cols, rows)
    return (input_grad, w1_grad, w3_grad, w2_grad)


def solution(mesh):
    in_specs = (
        P(("section", "hid"), "wid"),
        P(("section", "hid"), "wid"),
        P(("section", "wid"), "hid"),
        P(("section", "wid"), "hid"),
        P(("section", "hid", "wid"), None),
        P(("section", "hid", "wid")),
        P(("section", "hid", "wid"), None),
        P(("section", "hid", "wid")),
        P(("section", "hid", "wid"), None),
        P(("section", "hid", "wid")),
    )
    out_specs = (
        P(("section", "hid"), "wid"),
        P(("section", "hid", "wid"), None),
        P(("section", "hid", "wid"), None),
        P(("section", "hid", "wid"), None),
    )
    return jax.shard_map(body, mesh=mesh, in_specs=in_specs, out_specs=out_specs, check_vma=False)
```

profile of v0, /device:TPU:24, one launch (start us, length us, event | category | flops | bytes accessed | tf_op | source)
XLA Modules:
  0.0 429.0 jit_solution(11468545573826381574)
XLA Ops:
  7.2 2.7 collective-permute-start
  9.9 0.7 compare_select_fusion.2
  10.5 13.3 %all_gather.14 = bf16[128,448]{1,0:T(8,128)(2,1)S(1)} all-gather(bf16[16,448]{1,0:T(8,128)(2,1)} %param.12), channel_id=1, replica_groups=mesh['section'=4,'hid'=32,'wid'=8] {'wid'}, dimensions={0}, use_global_device_ids=true | all-gather | bytes 129024 | tf_op jit(solution)/shard_map/all_gather | solution.py:71
  23.8 0.7 compare_select_fusion.1
  24.5 0.7 compare_select_fusion
  25.1 74.4 %all-gather.1 = bf16[32,4,1024]{2,1,0:T(4,128)(2,1)} all-gather(bf16[1,4,1024]{2,1,0:T(4,128)(2,1)} %bitcast.55), channel_id=1, replica_groups=mesh['section'=4,'hid'=32,'wid'=8] {'hid'}, dimensions={0}, use_global_device_ids=true | all-gather | bytes 270336 | tf_op jit(solution)/shard_map/all_gather | solution.py:61
  99.6 13.0 %all_gather.13 = bf16[128,448]{1,0:T(8,128)(2,1)S(1)} all-gather(bf16[16,448]{1,0:T(8,128)(2,1)} %param.13), channel_id=1, replica_groups=mesh['section'=4,'hid'=32,'wid'=8] {'wid'}, dimensions={0}, use_global_device_ids=true | all-gather | bytes 129024 | tf_op jit(solution)/shard_map/all_gather | solution.py:72
  112.5 1.6 reshape.108
  114.1 0.5 broadcast.19.clone
  114.6 2.2 scatter_fusion
  116.9 1.2 copy.29
  118.1 2.1 reshape.64
  120.5 0.7 reshape.116
  121.3 0.5 broadcast.19.clone.1
  121.7 2.1 scatter_fusion.1
  123.9 1.4 slice.19
  125.3 3.5 copy.32
  128.8 2.1 reshape.67
  130.9 0.7 reshape.124
  131.6 0.5 broadcast.19.clone.2
  132.0 2.1 scatter_fusion.2
  134.2 1.4 slice.20
  135.6 3.5 copy.33
  139.1 1.3 reshape.70
  140.4 1.0 reshape.137
  141.4 52.8 %all-gather = bf16[32,4,1024]{2,1,0:T(4,128)(2,1)S(1)} all-gather(bf16[1,4,1024]{2,1,0:T(4,128)(2,1)S(1)} %bitcast.56), channel_id=1, replica_groups=mesh['section'=4,'hid'=32,'wid'=8] {'hid'}, dimensions={0}, use_global_device_ids=true | all-gather | bytes 270336 | tf_op jit(solution)/shard_map/all_gather | solution.py:60
  194.3 2.3 convolution_bitcast_fusion
  196.5 1.4 convolution_convert_fusion
  197.9 2.7 reshape.77
  200.7 0.5 copy.36
  201.2 1.8 concatenate.11
  202.9 2.3 gather_fusion.2
  205.2 1.3 reshape.79
  206.5 76.5 %all-reduce.6.cloned.1.call-done = f32[128,448]{0,1:T(8,128)} async-done(((f32[128,448]{0,1:T(8,128)}), f32[128,448]{0,1:T(8,128)}) %all-reduce.6.cloned.1.call-update) | async-done | bytes 229392 | tf_op jit(solution)/shard_map/psum | solution.py:69
  283.0 1.1 fusion.4
  284.8 115.6 %all-reduce.7 = bf16[128,1024]{1,0:T(8,128)(2,1)} all-reduce(f32[128,1024]{1,0:T(8,128)S(1)} %convolution_add_fusion), channel_id=1, replica_groups=mesh['section'=4,'hid'=32,'wid'=8] {'hid'}, use_global_device_ids=true, to_apply=%region_4.0 | all-reduce | flops 131072 | bytes 786432 | tf_op jit(solution)/shard_map/psum | solution.py:77
  400.8 1.2 reshape.71
  402.0 3.4 copy.34
  405.4 2.0 concatenate.9
  407.4 0.7 gather_fusion
  408.1 1.3 reshape.73
  409.4 0.4 fusion.1
  409.8 2.2 reshape.74
  411.9 3.7 copy.35
  415.6 1.8 concatenate.10
  417.4 2.2 gather_fusion.1
  419.6 1.3 reshape.76
  420.9 1.3 dynamic-slice_convert_fusion
  (21 shorter events, 1.7 us)
Async XLA Ops:
  7.2 275.8 %all-reduce.6.cloned.1.call-start = ((), (), s32[]{:S(2)}) async-start(), calls=%async_computation | async-start | bytes 458752 | tf_op jit(solution)/shard_map/psum | solution.py:69
  7.2 134.2 %collective-permute-start = (bf16[4,1024]{1,0:T(4,128)(2,1)}, bf16[4,1024]{1,0:T(4,128)(2,1)S(1)}, u32[]{:S(2)}, u32[]{:S(2)}) collective-permute-start(bf16[4,1024]{1,0:T(4,128)(2,1)} %param.10), channel_id=1, source_target_pairs={{0,768},{256,0},{512,256},{768,512},{1,769},{257,1},{513,257},{769... | collective-permute-start | bytes 24584 | tf_op jit(solution)/shard_map/ppermute | solution.py:11
  118.1 2.4 copy-start.2
  128.7 2.1 copy-start.3
  202.9 81.1 %copy-start = (bf16[1024,448]{0,1:T(8,128)(2,1)S(1)}, bf16[1024,448]{0,1:T(8,128)(2,1)}, u32[]{:S(2)}) copy-start(bf16[1024,448]{0,1:T(8,128)(2,1)} %reshape.67) | copy-start | bytes 2752516
  283.0 1.5 copy-start.1
Sparse Core Ops, SparseCore 0:
  196.7 86.2 all-reduce.5
where the time goes:
time: 430 us; the launch traced here: 429 us
  blocking collectives  269 us (63%)
  waiting for transfers between devices  76.5 us (18%)
  local copies, waits for them, and re-layouts  58.2 us (14%)
  between operations  14.3 us (3%)
  matrix products  5.14 us (1%)
    psum x1, blocking collectives, body(): lax.psum(total + jnp.einsum('tf,df->td', up_grad, third, preferred_elemen...  116 us
    psum x1, waiting for transfers between devices, body(): hidden_grad = lax.psum(partial_grad, 'wid')  76.5 us
    all_gather x1, blocking collectives, body(): lax.all_gather(inputs, 'hid', axis=0, tiled=True)  74.4 us
    all_gather x1, blocking collectives, body(): lax.all_gather(arrived, 'hid', axis=0, tiled=True)  52.8 us
    reshape x6, local copies, waits for them, and re-layouts, slots_from(): dense.reshape(rows, BLOCK, cols, BLOCK).transpose(0, 2, 1, 3)  13.6 us
    all_gather x1, blocking collectives, body(): lax.all_gather(gate_pre, 'wid', axis=0, tiled=True)  13.3 us
    all_gather x1, blocking collectives, body(): lax.all_gather(up_pre, 'wid', axis=0, tiled=True)  13 us
  transfers between devices with their start and end apart: 2, of which 1 were waited for; matrix products, arithmetic and copies ran while one was open for 9% of the time, Pallas kernels for 0%

commit v1 on v0

v1 whole, which is shorter than its diff:
```python
import functools

import jax
import jax.numpy as jnp
from jax import lax
from jax.experimental import pallas as pl
from jax.experimental.pallas import tpu as pltpu
from jax.sharding import PartitionSpec as P

BLOCK = 64
F32, BF16 = jnp.float32, jnp.bfloat16
NT = (((1,), (1,)), ((), ()))
TN = (((0,), (0,)), ((), ()))


def left_half(shape):
    return lax.broadcasted_iota(jnp.int32, shape, len(shape) - 1) < BLOCK


def unpack_blocks(values, spread, cap):
    mask = left_half((cap, 128))
    for pair in range(BLOCK // 2):
        rows = values[:, 128 * pair : 128 * pair + 128].astype(F32)
        turned = pltpu.roll(rows, BLOCK, 1)
        spread[pl.ds(2 * pair, cap, stride=BLOCK), :] = jnp.where(mask, rows, turned)
        spread[pl.ds(2 * pair + 1, cap, stride=BLOCK), :] = jnp.where(mask, turned, rows)


def place_blocks(index, spread, dense, cols, cap):
    lane = lax.broadcasted_iota(jnp.int32, (BLOCK, 128), 1) // BLOCK

    def step(slot, carry):
        number = index[slot]
        row = number // cols
        col = number - row * cols
        block = spread[pl.ds(pl.multiple_of(slot * BLOCK, BLOCK), BLOCK), :].astype(BF16)
        down = pl.ds(pl.multiple_of(row * BLOCK, BLOCK), BLOCK)
        along = pl.ds(pl.multiple_of(col // 2 * 128, 128), 128)
        old = dense[down, along]
        dense[down, along] = jnp.where(lane == col % 2, block, old)
        return carry

    lax.fori_loop(0, cap, step, 0, unroll=4)


def dense_kernel(index, values, dense, spread, *, cols):
    cap = values.shape[0]
    dense[...] = jnp.zeros_like(dense)
    unpack_blocks(values, spread, cap)
    place_blocks(index, spread, dense, cols, cap)


def take_blocks(index, dense, picked, cols, cap):
    def step(slot, carry):
        number = index[slot]
        row = number // cols
        col = number - row * cols
        down = pl.ds(pl.multiple_of(row * BLOCK, BLOCK), BLOCK)
        along = pl.ds(pl.multiple_of(col // 2 * 128, 128), 128)
        block = pltpu.roll(dense[down, along], col % 2 * BLOCK, 1)
        picked[pl.ds(pl.multiple_of(slot * BLOCK, BLOCK), BLOCK), :] = block
        return carry

    lax.fori_loop(0, cap, step, 0, unroll=4)


def pack_blocks(picked, out, cap):
    mask = left_half((cap, 128))
    for pair in range(BLOCK // 2):
        upper = picked[pl.ds(2 * pair, cap, stride=BLOCK), :]
        lower = pltpu.roll(picked[pl.ds(2 * pair + 1, cap, stride=BLOCK), :], BLOCK, 1)
        out[:, 128 * pair : 128 * pair + 128] = jnp.where(mask, upper, lower).astype(BF16)


def hidden_kernel(tokens, dense, out):
    prod = lax.dot_general(tokens[...], dense[...], NT, preferred_element_type=F32)
    width = prod.shape[1]
    top = lax.broadcasted_iota(jnp.int32, (8, width), 0) < 4
    half = prod.shape[0] // 2
    for k in range(half // 8):
        even = prod[8 * k : 8 * k + 8]
        odd = prod[half + 8 * k : half + 8 * k + 8]
        out[8 * k : 8 * k + 8, :] = jnp.where(top, even, pltpu.roll(odd, 4, 0))


def gate_kernel(parts, gate, up, out):
    width = gate.shape[1]
    total = parts[0]
    for i in range(1, parts.shape[0]):
        total = total + parts[i]
    hidden = total[:, :width]
    g = gate[...].astype(F32)
    u = up[...].astype(F32)
    sigma = 1.0 / (1.0 + jnp.exp(-g))
    gate_grad = (hidden * u * sigma * (1.0 + g * (1.0 - sigma))).astype(BF16)
    up_grad = (hidden * g * sigma).astype(BF16)
    activ = (g * sigma * u).astype(BF16)
    out[...] = jnp.zeros_like(out)
    for peer in range(out.shape[0]):
        out[peer, 0, :, :width] = gate_grad
        out[peer, 1, :, :width] = up_grad
        out[peer, 2, :, :width] = activ


def all_rows(acts, which):
    picked = acts[:, which]
    return picked.reshape(picked.shape[0] * picked.shape[1], picked.shape[2])


def input_kernel(acts, d1, d3, out):
    half = out.shape[1]
    rows = 2 * half
    prod = lax.dot_general(all_rows(acts, 0), d1[:rows], NT, preferred_element_type=F32)
    prod = prod + lax.dot_general(all_rows(acts, 1), d3[:rows], NT, preferred_element_type=F32)
    top = lax.broadcasted_iota(jnp.int32, (8, half), 0) < 4
    across = out.shape[0] // 32

    def folded(peer):
        tile = prod[8 * (peer // 2) : 8 * (peer // 2) + 8]
        left, right = tile[:, :half], tile[:, half:]
        if peer % 2:
            return jnp.where(top, pltpu.roll(left, 4, 0), right)
        return jnp.where(top, left, pltpu.roll(right, 4, 0))

    for q in range(4):
        for b in range(0, across, 2):
            base = (q * across + b) * 8
            both = [folded(4 * b + q), folded(4 * b + 4 + q)]
            out[base : base + 16, :] = jnp.concatenate(both, 0).astype(BF16)


def near_kernel(parts, out):
    total = parts[0].astype(F32)
    for i in range(1, parts.shape[0]):
        total = total + parts[i].astype(F32)
    out[...] = total.astype(BF16)


def far_kernel(parts, out):
    total = parts[0].astype(F32)
    for i in range(1, parts.shape[0]):
        total = total + parts[i].astype(F32)
    half = total.shape[1]
    out[:, :half] = total[:4].astype(BF16)
    out[:, half:] = pltpu.roll(total, 4, 0)[:4].astype(BF16)


def weight_kernel(i1, i3, i2, tokens, acts, o1, o3, o2, spaced, dense, tall, picked, *, rows, cols):
    cap = o1.shape[0]
    count, width = acts.shape[0] * acts.shape[2], acts.shape[3]
    top = lax.broadcasted_iota(jnp.int32, (8, width), 0) < 4
    zero = jnp.zeros((8, width), F32)

    def spread_rows(which, upper):
        full = all_rows(acts, which).astype(F32)
        for k in range(count // 8):
            piece = full[8 * k : 8 * k + 8]
            turned = pltpu.roll(piece, 4, 0)
            if upper:
                even, odd = jnp.where(top, piece, zero), jnp.where(top, turned, zero)
            else:
                even, odd = jnp.where(top, zero, turned), jnp.where(top, zero, piece)
            spaced[8 * k : 8 * k + 8, :] = even
            spaced[count + 8 * k : count + 8 * k + 8, :] = odd
        return spaced[...].astype(BF16)

    dense[rows * BLOCK :, :] = jnp.zeros((BLOCK, width), F32)
    for which, index, out in ((0, i1, o1), (1, i3, o3)):
        dense[: rows * BLOCK, :] = lax.dot_general(
            tokens[...], spread_rows(which, False), TN, preferred_element_type=F32)
        take_blocks(index, dense, picked, cols, cap)
        pack_blocks(picked, out, cap)
    tall[...] = lax.dot_general(spread_rows(2, True), tokens[...], TN, preferred_element_type=F32)
    take_blocks(i2, tall, picked, rows, cap)
    pack_blocks(picked, o2, cap)


def vm():
    return pl.BlockSpec(memory_space=pltpu.VMEM)


def sm():
    return pl.BlockSpec(memory_space=pltpu.SMEM)


def densify(index, values, rows, cols):
    cap = values.shape[0]
    wide = (cols + 1) // 2 * 128
    return pl.pallas_call(
        functools.partial(dense_kernel, cols=cols),
        out_shape=jax.ShapeDtypeStruct((rows * BLOCK + BLOCK, wide), BF16),
        in_specs=[sm(), vm()],
        out_specs=vm(),
        scratch_shapes=[pltpu.VMEM((cap * BLOCK, 128), F32)],
        name="densify",
    )(index, values)


def hidden(tokens, d2):
    return pl.pallas_call(hidden_kernel, out_shape=jax.ShapeDtypeStruct((tokens.shape[0] // 2, d2.shape[0]), F32),
        in_specs=[vm()] * 2, out_specs=vm(), name="hidden")(tokens, d2)


def gate(parts, g, u):
    return pl.pallas_call(gate_kernel, out_shape=jax.ShapeDtypeStruct((parts.shape[0], 3) + parts.shape[1:], BF16),
        in_specs=[vm()] * 3, out_specs=vm(), name="gate")(parts, g, u)


def inputg(acts, d1, d3, width):
    tokens = acts.shape[0] * acts.shape[2]
    return pl.pallas_call(
        input_kernel,
        out_shape=jax.ShapeDtypeStruct((2 * tokens, width // 2), BF16),
        in_specs=[vm()] * 3,
        out_specs=vm(),
        name="inputg",
    )(acts, d1, d3)


def near_sum(parts):
    return pl.pallas_call(
        near_kernel,
        out_shape=jax.ShapeDtypeStruct(parts.shape[1:], BF16),
        in_specs=[vm()],
        out_specs=vm(),
        name="near_sum",
    )(parts)


def far_sum(parts):
    return pl.pallas_call(
        far_kernel,
        out_shape=jax.ShapeDtypeStruct((parts.shape[1] // 2, 2 * parts.shape[2]), BF16),
        in_specs=[vm()],
        out_specs=vm(),
        name="far_sum",
    )(parts)


def weights(i1, i3, i2, tokens, acts, rows, cols):
    cap = i1.shape[0]
    wide = acts.shape[3]
    count = acts.shape[0] * acts.shape[2]
    o = jax.ShapeDtypeStruct((cap, BLOCK * BLOCK), BF16)
    return pl.pallas_call(
        functools.partial(weight_kernel, rows=rows, cols=cols), out_shape=(o, o, o),
        in_specs=[sm()] * 3 + [vm()] * 2, out_specs=(vm(),) * 3,
        scratch_shapes=[pltpu.VMEM((2 * count, wide), F32), pltpu.VMEM((rows * BLOCK + BLOCK, wide), F32),
            pltpu.VMEM((wide, rows * BLOCK), F32), pltpu.VMEM((cap * BLOCK, 128), F32)],
        name="weights")(i1, i3, i2, tokens, acts)


def strided(peers, by):
    return [list(range(first, peers, by)) for first in range(by)]


def adjacent(peers, many):
    return [list(range(first, first + many)) for first in range(0, peers, many)]


def gather_tokens(both):
    peers = lax.axis_size("hid")
    skipping = lax.all_gather(both, "hid", axis=0, tiled=True, axis_index_groups=strided(peers, 2))
    return lax.all_gather(skipping, "hid", axis=0, tiled=True, axis_index_groups=adjacent(peers, 2))


def exchange(chunks, groups):
    return lax.all_to_all(chunks, "hid", 0, 0, tiled=True, axis_index_groups=groups)


def scatter_sum(total):
    peers = lax.axis_size("hid")
    width = total.shape[1]
    near = near_sum(exchange(total.reshape(4, -1, width), adjacent(peers, 4)))
    return far_sum(exchange(near.reshape(peers // 4, -1, width), strided(peers, 4)))


def body(
    out_grad,
    inputs,
    gate_pre,
    up_pre,
    w1_values,
    w1_index,
    w3_values,
    w3_index,
    w2_values,
    w2_index,
):
    rows = inputs.shape[1] // BLOCK
    cols = gate_pre.shape[1] // BLOCK
    sections = lax.axis_size("section")
    arrived = lax.ppermute(out_grad, "section", [(i, (i - 1) % sections) for i in range(sections)])
    tokens = gather_tokens(jnp.concatenate([arrived, inputs], axis=0))
    second = densify(w2_index, w2_values, cols, rows)
    first = densify(w1_index, w1_values, rows, cols)
    third = densify(w3_index, w3_values, rows, cols)
    partial_grad = hidden(tokens, second)
    peers = lax.axis_size("wid")
    parts = partial_grad.reshape(peers, partial_grad.shape[0] // peers, partial_grad.shape[1])
    parts = lax.all_to_all(parts, "wid", 0, 0, tiled=True)
    acts = lax.all_to_all(gate(parts, gate_pre, up_pre), "wid", 0, 0, tiled=True)
    input_grad = scatter_sum(inputg(acts, first, third, inputs.shape[1]))
    w1_grad, w3_grad, w2_grad = weights(w1_index, w3_index, w2_index, tokens, acts, rows, cols)
    return (input_grad, w1_grad, w3_grad, w2_grad)


def solution(mesh):
    in_specs = (
        P(("section", "hid"), "wid"),
        P(("section", "hid"), "wid"),
        P(("section", "wid"), "hid"),
        P(("section", "wid"), "hid"),
        P(("section", "hid", "wid"), None),
        P(("section", "hid", "wid")),
        P(("section", "hid", "wid"), None),
        P(("section", "hid", "wid")),
        P(("section", "hid", "wid"), None),
        P(("section", "hid", "wid")),
    )
    out_specs = (
        P(("section", "hid"), "wid"),
        P(("section", "hid", "wid"), None),
        P(("section", "hid", "wid"), None),
        P(("section", "hid", "wid"), None),
    )
    return jax.shard_map(body, mesh=mesh, in_specs=in_specs, out_specs=out_specs, check_vma=False)
```

time: 430 us -> 151 us (0.35)
  blocking collectives: 269 us -> 70.5 us
  local copies, waits for them, and re-layouts: 58.2 us -> 1.38 us
  waiting for transfers between devices: 76.5 us -> 26.3 us
  Pallas kernels: 0 us -> 30.5 us
  starting transfers between devices: 2.69 us -> 18.7 us
  between operations: 14.3 us -> 0.67 us
  matrix products: 5.14 us -> 0 us
    psum x1 -> x0, blocking collectives: 116 us -> none  [body(): lax.psum(total + jnp.einsum('tf,df->td', up_grad, third, preferred_elemen...]
    all_gather x4 -> x2, blocking collectives: 153 us -> 45.9 us  [the longest x1 38.7 us: gather_tokens(): lax.all_gather(both, 'hid', axis=0, tiled=True, axis_index_groups=strided...]
    psum x1 -> x0, waiting for transfers between devices: 76.5 us -> none  [body(): hidden_grad = lax.psum(partial_grad, 'wid')]
    pallas_call x0 -> x9, Pallas kernels: none -> 30.5 us  [the longest x3 11 us: densify(): pl.pallas_call(functools.partial(dense_kernel, cols=cols), out_shape=jax....]
    reshape x15 -> x0, local copies, waits for them, and re-layouts: 25.9 us -> none  [the longest x6 13.6 us: slots_from(): dense.reshape(rows, BLOCK, cols, BLOCK).transpose(0, 2, 1, 3)]
    all_to_all x0 -> x2, blocking collectives: none -> 24.6 us  [the longest x1 12.7 us: exchange(): lax.all_to_all(chunks, 'hid', 0, 0, tiled=True, axis_index_groups=groups)]
    all_to_all x0 -> x2, waiting for transfers between devices: none -> 16.1 us  [the longest x1 14.6 us: exchange(): lax.all_to_all(chunks, 'hid', 0, 0, tiled=True, axis_index_groups=groups)]
    all_to_all x0 -> x2, starting transfers between devices: none -> 16 us  [the longest x1 12.6 us: exchange(): lax.all_to_all(chunks, 'hid', 0, 0, tiled=True, axis_index_groups=groups)]
  transfers between devices with their start and end apart: 2 -> 3, of which waited for: 1 -> 3; matrix products, arithmetic and copies ran while one was open for 9% -> 0% of each run, Pallas kernels for 0% -> 13%
where the time goes in v1:
time: 151 us; the launch traced here: 148 us
  blocking collectives  70.5 us (47%)
  Pallas kernels  30.5 us (20%)
  waiting for transfers between devices  26.3 us (17%)
  starting transfers between devices  18.7 us (12%)
    all_gather x1, blocking collectives, gather_tokens(): lax.all_gather(both, 'hid', axis=0, tiled=True, axis_index_groups=strided...  38.7 us
    all_to_all x1, waiting for transfers between devices, exchange(): lax.all_to_all(chunks, 'hid', 0, 0, tiled=True, axis_index_groups=groups)  14.6 us
    all_to_all x1, blocking collectives, exchange(): lax.all_to_all(chunks, 'hid', 0, 0, tiled=True, axis_index_groups=groups)  12.7 us
    all_to_all x1, starting transfers between devices, exchange(): lax.all_to_all(chunks, 'hid', 0, 0, tiled=True, axis_index_groups=groups)  12.6 us
    all_to_all x1, blocking collectives, body(): parts = lax.all_to_all(parts, 'wid', 0, 0, tiled=True)  11.9 us
    pallas_call x3, Pallas kernels, densify(): pl.pallas_call(functools.partial(dense_kernel, cols=cols), out_shape=jax....  11 us
    ppermute x1, waiting for transfers between devices, body(): lax.ppermute(out_grad, 'section', [(i, (i - 1) % sections) for i in range...  10.3 us
    pallas_call x1, Pallas kernels, weights(): pl.pallas_call(functools.partial(weight_kernel, rows=rows, cols=cols), ou...  8.87 us
  transfers between devices with their start and end apart: 3, of which 3 were waited for; matrix products, arithmetic and copies ran while one was open for 0% of the time, Pallas kernels for 13%

profile of v1, /device:TPU:24, one launch (start us, length us, event | category | flops | bytes accessed | tf_op | source)
XLA Modules:
  0.0 148.1 jit_solution(17651710727317655849)
XLA Ops:
  0.6 0.0 copy-start.2
  0.6 2.7 %collective-permute-start = (bf16[4,1024]{1,0:T(4,128)(2,1)}, bf16[4,1024]{1,0:T(4,128)(2,1)S(1)}, u32[]{:S(2)}, u32[]{:S(2)}) collective-permute-start(bf16[4,1024]{1,0:T(4,128)(2,1)} %param.10), channel_id=1, source_target_pairs={{0,768},{256,0},{512,256},{768,512},{1,769},{257,1},{513,257},{769... | collective-permute-start | bytes 24584 | tf_op jit(solution)/shard_map/ppermute | solution.py:293
  3.3 3.6 %densify.3.dense = bf16[512,1024]{1,0:T(8,128)(2,1)} custom-call(s32[40]{0:T(128)} %i2.1, bf16[40,4096]{1,0:T(8,128)(2,1)} %values.3), custom_call_target="tpu_custom_call" | custom-call | tf_op jit(solution)/shard_map/densify/pallas_call | solution.py:189
  6.9 10.3 %collective-permute-done = bf16[4,1024]{1,0:T(4,128)(2,1)S(1)} collective-permute-done((bf16[4,1024]{1,0:T(4,128)(2,1)}, bf16[4,1024]{1,0:T(4,128)(2,1)S(1)}, u32[]{:S(2)}, u32[]{:S(2)}) %collective-permute-start) | collective-permute-done | bytes 8224 | tf_op jit(solution)/shard_map/ppermute | solution.py:293
  17.2 0.0 copy-done.2
  17.2 38.7 %all_gather.6 = bf16[128,1024]{1,0:T(8,128)(2,1)S(1)} all-gather(bf16[8,1024]{1,0:T(8,128)(2,1)S(1)} %pad_maximum_fusion), channel_id=1, replica_groups={{0,16,32,48,64,80,96,112,128,144,160,176,192,208,224,240},{8,24,40,56,7..., dimensions={0}, use_global_device_ids=true | all-gather | bytes 278528 | tf_op jit(solution)/shard_map/all_gather | solution.py:263
  56.0 7.1 %all_gather.7.tokens = bf16[256,1024]{1,0:T(8,128)(2,1)} all-gather(bf16[128,1024]{1,0:T(8,128)(2,1)S(1)} %all_gather.6), channel_id=1, replica_groups={{0,8},{16,24},{32,40},{48,56},{64,72},{80,88},{96,104},{112,120},{128,1..., dimensions={0}, use_global_device_ids=true | all-gather | bytes 786432 | tf_op jit(solution)/shard_map/all_gather | solution.py:264
  63.1 2.6 %hidden.1 = f32[128,512]{1,0:T(8,128)} custom-call(bf16[256,1024]{1,0:T(8,128)(2,1)} %all_gather.7.tokens, bf16[512,1024]{1,0:T(8,128)(2,1)} %densify.3.dense), custom_call_target="tpu_custom_call" | custom-call | tf_op jit(solution)/shard_map/hidden/pallas_call | solution.py:200
  65.7 11.9 %all_to_all.20.parts = f32[8,16,512]{2,1,0:T(8,128)} all-to-all(f32[8,16,512]{2,1,0:T(8,128)} %bitcast.3), channel_id=1, replica_groups=mesh['section'=4,'hid'=32,'wid'=8] {'wid'}, dimensions={0} | all-to-all | bytes 524288 | tf_op jit(solution)/shard_map/all_to_all | solution.py:301
  77.6 1.8 %gate.2 = bf16[8,3,16,512]{3,2,1,0:T(8,128)(2,1)} custom-call(f32[8,16,512]{2,1,0:T(8,128)} %all_to_all.20.parts, bf16[16,448]{1,0:T(8,128)(2,1)} %gate.3, bf16[16,448]{1,0:T(8,128)(2,1)} %up.1), custom_call_target="tpu_custom_call" | custom-call | tf_op jit(solution)/shard_map/gate/pallas_call | solution.py:205
  79.4 3.5 %all-to-all-start.1 = ((bf16[8,3,16,512]{3,2,1,0:T(8,128)(2,1)}), bf16[8,3,16,512]{3,2,1,0:T(8,128)(2,1)S(1)}, u32[]{:S(2)}, u32[]{:S(2)}) async-start(bf16[8,3,16,512]{3,2,1,0:T(8,128)(2,1)} %gate.2), calls=%async_computation.1 | async-start | bytes 786432 | tf_op jit(solution)/shard_map/all_to_all | solution.py:302
  82.8 3.7 %densify.4.d1 = bf16[1088,512]{1,0:T(8,128)(2,1)} custom-call(s32[40]{0:T(128)} %i1.1, bf16[40,4096]{1,0:T(8,128)(2,1)} %values.4), custom_call_target="tpu_custom_call" | custom-call | tf_op jit(solution)/shard_map/densify/pallas_call | solution.py:189
  86.5 3.7 %densify.5.d3 = bf16[1088,512]{1,0:T(8,128)(2,1)} custom-call(s32[40]{0:T(128)} %i3.1, bf16[40,4096]{1,0:T(8,128)(2,1)} %values.5), custom_call_target="tpu_custom_call" | custom-call | tf_op jit(solution)/shard_map/densify/pallas_call | solution.py:189
  90.2 1.5 all-to-all-done.1.acts
  91.7 0.0 copy-start
  91.7 0.7 copy-done
  92.4 3.2 %inputg.1 = bf16[256,512]{1,0:T(8,128)(2,1)} custom-call(bf16[8,3,16,512]{3,2,1,0:T(8,128)(2,1)} %copy-done, bf16[1088,512]{1,0:T(8,128)(2,1)} %densify.4.d1, bf16[1088,512]{1,0:T(8,128)(2,1)} %densify.5.d3), custom_call_target="tpu_custom_call" | custom-call | tf_op jit(solution)/shard_map/inputg/pallas_call | solution.py:211
  95.6 12.7 %all_to_all.21.parts = bf16[4,64,512]{2,1,0:T(8,128)(2,1)} all-to-all(bf16[4,64,512]{2,1,0:T(8,128)(2,1)} %bitcast.4), channel_id=1, replica_groups={{0,8,16,24},{32,40,48,56},{64,72,80,88},{96,104,112,120},{128,136,144,1..., dimensions={0} | all-to-all | bytes 524288 | tf_op jit(solution)/shard_map/all_to_all | solution.py:268
  108.4 1.6 %near_sum.1 = bf16[64,512]{1,0:T(8,128)(2,1)} custom-call(bf16[4,64,512]{2,1,0:T(8,128)(2,1)} %all_to_all.21.parts), custom_call_target="tpu_custom_call" | custom-call | tf_op jit(solution)/shard_map/near_sum/pallas_call | solution.py:221
  110.0 12.6 %all-to-all-start.3 = ((bf16[8,8,512]{2,1,0:T(8,128)(2,1)}), bf16[8,8,512]{2,1,0:T(8,128)(2,1)S(1)}, u32[]{:S(2)}, u32[]{:S(2)}) async-start(bf16[8,8,512]{2,1,0:T(8,128)(2,1)} %bitcast.5), calls=%async_computation.3 | async-start | bytes 131072 | tf_op jit(solution)/shard_map/all_to_all | solution.py:268
  122.5 8.9 %weights.1 = (bf16[40,4096]{1,0:T(8,128)(2,1)}, bf16[40,4096]{1,0:T(8,128)(2,1)}, bf16[40,4096]{1,0:T(8,128)(2,1)}) custom-call(s32[40]{0:T(128)} %i1.1, s32[40]{0:T(128)} %i3.1, s32[40]{0:T(128)} %i2.1, bf16[256,1024]{1,0:T(8,128)(2,1)} %all_gather.7.tokens, bf16[8,3,16,512]{3,2,1,0:T(8,128)(2,1)} %copy-done), custom_call_target="tpu_custom_call" | custom-call | tf_op jit(solution)/shard_map/weights/pallas_call | solution.py:245
  131.4 14.6 %all-to-all-done.3.parts = bf16[8,8,512]{2,1,0:T(8,128)(2,1)S(1)} async-done(((bf16[8,8,512]{2,1,0:T(8,128)(2,1)}), bf16[8,8,512]{2,1,0:T(8,128)(2,1)S(1)}, u32[]{:S(2)}, u32[]{:S(2)}) %all-to-all-start.3) | async-done | bytes 65568 | tf_op jit(solution)/shard_map/all_to_all | solution.py:268
  146.0 0.0 copy-start.1
  146.0 0.6 copy-done.1
  146.6 1.5 far_sum.1
  (1 shorter events, 0.0 us)
Async XLA Ops:
  0.6 16.6 %copy-start.2 = (bf16[4,1024]{1,0:T(4,128)(2,1)S(1)}, bf16[4,1024]{1,0:T(4,128)(2,1)}, u32[]{:S(2)}) copy-start(bf16[4,1024]{1,0:T(4,128)(2,1)} %param.11) | copy-start | bytes 24580
  0.6 16.6 %collective-permute-start = (bf16[4,1024]{1,0:T(4,128)(2,1)}, bf16[4,1024]{1,0:T(4,128)(2,1)S(1)}, u32[]{:S(2)}, u32[]{:S(2)}) collective-permute-start(bf16[4,1024]{1,0:T(4,128)(2,1)} %param.10), channel_id=1, source_target_pairs={{0,768},{256,0},{512,256},{768,512},{1,769},{257,1},{513,257},{769... | collective-permute-start | bytes 24584 | tf_op jit(solution)/shard_map/ppermute | solution.py:293
  79.4 12.3 %all-to-all-start.1 = ((bf16[8,3,16,512]{3,2,1,0:T(8,128)(2,1)}), bf16[8,3,16,512]{3,2,1,0:T(8,128)(2,1)S(1)}, u32[]{:S(2)}, u32[]{:S(2)}) async-start(bf16[8,3,16,512]{3,2,1,0:T(8,128)(2,1)} %gate.2), calls=%async_computation.1 | async-start | bytes 786432 | tf_op jit(solution)/shard_map/all_to_all | solution.py:302
  91.7 0.7 copy-start
  110.0 36.0 %all-to-all-start.3 = ((bf16[8,8,512]{2,1,0:T(8,128)(2,1)}), bf16[8,8,512]{2,1,0:T(8,128)(2,1)S(1)}, u32[]{:S(2)}, u32[]{:S(2)}) async-start(bf16[8,8,512]{2,1,0:T(8,128)(2,1)} %bitcast.5), calls=%async_computation.3 | async-start | bytes 131072 | tf_op jit(solution)/shard_map/all_to_all | solution.py:268
  146.0 0.6 copy-start.1

commit v2 on v1

--- a/solution.py
+++ b/solution.py
@@ -8,6 +8,7 @@
 from jax.sharding import PartitionSpec as P
 
 BLOCK = 64
+GRANT = 16 << 20
 F32, BF16 = jnp.float32, jnp.bfloat16
 NT = (((1,), (1,)), ((), ()))
 TN = (((0,), (0,)), ((), ()))
@@ -83,7 +84,8 @@
         out[8 * k : 8 * k + 8, :] = jnp.where(top, even, pltpu.roll(odd, 4, 0))
 
 
-def gate_kernel(parts, gate, up, out):
+def gate_kernel(parts, gate, up, after, out):
+    del after
     width = gate.shape[1]
     total = parts[0]
     for i in range(1, parts.shape[0]):
@@ -179,6 +181,14 @@
     return pl.BlockSpec(memory_space=pltpu.VMEM)
 
 
+def near(*arrays):
+    return tuple(pltpu.with_memory_space_constraint(a, pltpu.VMEM) for a in arrays)
+
+
+def on_chip(shape, dtype):
+    return pltpu.VMEM(shape, dtype)
+
+
 def sm():
     return pl.BlockSpec(memory_space=pltpu.SMEM)
 
@@ -188,43 +198,58 @@
     wide = (cols + 1) // 2 * 128
     return pl.pallas_call(
         functools.partial(dense_kernel, cols=cols),
-        out_shape=jax.ShapeDtypeStruct((rows * BLOCK + BLOCK, wide), BF16),
+        out_shape=on_chip((rows * BLOCK + BLOCK, wide), BF16),
         in_specs=[sm(), vm()],
         out_specs=vm(),
         scratch_shapes=[pltpu.VMEM((cap * BLOCK, 128), F32)],
+        compiler_params=pltpu.CompilerParams(vmem_limit_bytes=GRANT),
         name="densify",
     )(index, values)
 
 
 def hidden(tokens, d2):
-    return pl.pallas_call(hidden_kernel, out_shape=jax.ShapeDtypeStruct((tokens.shape[0] // 2, d2.shape[0]), F32),
-        in_specs=[vm()] * 2, out_specs=vm(), name="hidden")(tokens, d2)
-
-
-def gate(parts, g, u):
-    return pl.pallas_call(gate_kernel, out_shape=jax.ShapeDtypeStruct((parts.shape[0], 3) + parts.shape[1:], BF16),
-        in_specs=[vm()] * 3, out_specs=vm(), name="gate")(parts, g, u)
+    return pl.pallas_call(
+        hidden_kernel,
+        out_shape=on_chip((tokens.shape[0] // 2, d2.shape[0]), F32),
+        in_specs=[vm()] * 2,
+        out_specs=vm(),
+        compiler_params=pltpu.CompilerParams(vmem_limit_bytes=GRANT),
+        name="hidden",
+    )(*near(tokens, d2))
+
+
+def gate(parts, gate_pre, up_pre, after):
+    return pl.pallas_call(
+        gate_kernel,
+        out_shape=on_chip((parts.shape[0], 3) + parts.shape[1:], BF16),
+        in_specs=[vm()] * 4,
+        out_specs=vm(),
+        compiler_params=pltpu.CompilerParams(vmem_limit_bytes=GRANT),
+        name="gate",
+    )(*near(parts), gate_pre, up_pre, *near(after))
 
 
 def inputg(acts, d1, d3, width):
     tokens = acts.shape[0] * acts.shape[2]
     return pl.pallas_call(
         input_kernel,
-        out_shape=jax.ShapeDtypeStruct((2 * tokens, width // 2), BF16),
+        out_shape=on_chip((2 * tokens, width // 2), BF16),
         in_specs=[vm()] * 3,
         out_specs=vm(),
+        compiler_params=pltpu.CompilerParams(vmem_limit_bytes=GRANT),
         name="inputg",
-    )(acts, d1, d3)
+    )(*near(acts, d1, d3))
 
 
 def near_sum(parts):
     return pl.pallas_call(
         near_kernel,
-        out_shape=jax.ShapeDtypeStruct(parts.shape[1:], BF16),
+        out_shape=on_chip(parts.shape[1:], BF16),
         in_specs=[vm()],
         out_specs=vm(),
+        compiler_params=pltpu.CompilerParams(vmem_limit_bytes=GRANT),
         name="near_sum",
-    )(parts)
+    )(*near(parts))
 
 
 def far_sum(parts):
@@ -233,8 +258,9 @@
         out_shape=jax.ShapeDtypeStruct((parts.shape[1] // 2, 2 * parts.shape[2]), BF16),
         in_specs=[vm()],
         out_specs=vm(),
+        compiler_params=pltpu.CompilerParams(vmem_limit_bytes=GRANT),
         name="far_sum",
-    )(parts)
+    )(*near(parts))
 
 
 def weights(i1, i3, i2, tokens, acts, rows, cols):
@@ -247,7 +273,7 @@
         in_specs=[sm()] * 3 + [vm()] * 2, out_specs=(vm(),) * 3,
         scratch_shapes=[pltpu.VMEM((2 * count, wide), F32), pltpu.VMEM((rows * BLOCK + BLOCK, wide), F32),
             pltpu.VMEM((wide, rows * BLOCK), F32), pltpu.VMEM((cap * BLOCK, 128), F32)],
-        name="weights")(i1, i3, i2, tokens, acts)
+        compiler_params=pltpu.CompilerParams(vmem_limit_bytes=GRANT), name="weights")(i1, i3, i2, *near(tokens, acts))
 
 
 def strided(peers, by):
@@ -299,7 +325,7 @@
     peers = lax.axis_size("wid")
     parts = partial_grad.reshape(peers, partial_grad.shape[0] // peers, partial_grad.shape[1])
     parts = lax.all_to_all(parts, "wid", 0, 0, tiled=True)
-    acts = lax.all_to_all(gate(parts, gate_pre, up_pre), "wid", 0, 0, tiled=True)
+    acts = lax.all_to_all(gate(parts, gate_pre, up_pre, third), "wid", 0, 0, tiled=True)
     input_grad = scatter_sum(inputg(acts, first, third, inputs.shape[1]))
     w1_grad, w3_grad, w2_grad = weights(w1_index, w3_index, w2_index, tokens, acts, rows, cols)
     return (input_grad, w1_grad, w3_grad, w2_grad)

time: 151 us -> 140 us (0.927)
  blocking collectives: 70.5 us -> 56.7 us
  Pallas kernels: 30.5 us -> 19 us
  waiting for transfers between devices: 26.3 us -> 36.8 us
  starting transfers between devices: 18.7 us -> 23.4 us
    all_to_all x1 -> x0, blocking collectives: 11.9 us -> none  [body(): parts = lax.all_to_all(parts, 'wid', 0, 0, tiled=True)]
    all_to_all x1 -> x2, waiting for transfers between devices: 1.47 us -> 11.8 us  [the longest x1 6.57 us: body(): lax.all_to_all(gate(parts, gate_pre, up_pre, third), 'wid', 0, 0, tiled=T...]
    pallas_call x7, Pallas kernels: 20.2 us -> 10.2 us  [the longest x3 6.7 us: densify(): pl.pallas_call(functools.partial(dense_kernel, cols=cols), out_shape=on_c...]
    all_to_all x1 -> x2, starting transfers between devices: 3.45 us -> 7.88 us  [the longest x1 4.43 us: body(): parts = lax.all_to_all(parts, 'wid', 0, 0, tiled=True)]
    all_to_all x1, blocking collectives: 12.7 us -> 11 us  [exchange(): lax.all_to_all(chunks, 'hid', 0, 0, tiled=True, axis_index_groups=groups)]
  transfers between devices with their start and end apart: 3 -> 4, of which waited for: 3 -> 4; matrix products, arithmetic and copies ran while one was open for 0% -> 0% of each run, Pallas kernels for 13% -> 11%
where the time goes in v2:
time: 140 us; the launch traced here: 138 us
  blocking collectives  56.7 us (40%)
  waiting for transfers between devices  36.8 us (26%)
  starting transfers between devices  23.4 us (17%)
  Pallas kernels  19 us (14%)
  local copies, waits for them, and re-layouts  1.66 us (1%)
    all_gather x1, blocking collectives, gather_tokens(): lax.all_gather(both, 'hid', axis=0, tiled=True, axis_index_groups=strided...  38.7 us
    all_to_all x1, waiting for transfers between devices, exchange(): lax.all_to_all(chunks, 'hid', 0, 0, tiled=True, axis_index_groups=groups)  15 us
    all_to_all x1, starting transfers between devices, exchange(): lax.all_to_all(chunks, 'hid', 0, 0, tiled=True, axis_index_groups=groups)  12.8 us
    all_to_all x1, blocking collectives, exchange(): lax.all_to_all(chunks, 'hid', 0, 0, tiled=True, axis_index_groups=groups)  11 us
    ppermute x1, waiting for transfers between devices, body(): lax.ppermute(out_grad, 'section', [(i, (i - 1) % sections) for i in range...  10 us
    pallas_call x1, Pallas kernels, weights(): pl.pallas_call(functools.partial(weight_kernel, rows=rows, cols=cols), ou...  8.26 us
    all_gather x1, blocking collectives, gather_tokens(): lax.all_gather(skipping, 'hid', axis=0, tiled=True, axis_index_groups=adj...  7.03 us
    pallas_call x3, Pallas kernels, densify(): pl.pallas_call(functools.partial(dense_kernel, cols=cols), out_shape=on_c...  6.7 us
  transfers between devices with their start and end apart: 4, of which 4 were waited for; matrix products, arithmetic and copies ran while one was open for 0% of the time, Pallas kernels for 11%

profile of v2, /device:TPU:24, one launch (start us, length us, event | category | flops | bytes accessed | tf_op | source)
XLA Modules:
  0.0 138.4 jit_solution(12792037201030020179)
XLA Ops:
  0.6 2.7 %collective-permute-start = (bf16[4,1024]{1,0:T(4,128)(2,1)}, bf16[4,1024]{1,0:T(4,128)(2,1)S(1)}, u32[]{:S(2)}, u32[]{:S(2)}) collective-permute-start(bf16[4,1024]{1,0:T(4,128)(2,1)} %param.10), channel_id=1, source_target_pairs={{0,768},{256,0},{512,256},{768,512},{1,769},{257,1},{513,257},{769... | collective-permute-start | bytes 24584 | tf_op jit(solution)/shard_map/ppermute | solution.py:319
  3.3 0.0 copy-start
  3.3 1.0 copy-done
  4.3 0.0 copy-start.5
  4.3 0.7 copy-done.5
  4.9 0.0 copy-start.9
  4.9 2.2 %densify.3.dense = bf16[512,1024]{1,0:T(8,128)(2,1)S(1)} custom-call(s32[40]{0:T(128)S(1)} %copy-done.5, bf16[40,4096]{1,0:T(8,128)(2,1)S(1)} %copy-done), custom_call_target="tpu_custom_call" | custom-call | tf_op jit(solution)/shard_map/densify/pallas_call | solution.py:199
  7.2 10.0 %collective-permute-done = bf16[4,1024]{1,0:T(4,128)(2,1)S(1)} collective-permute-done((bf16[4,1024]{1,0:T(4,128)(2,1)}, bf16[4,1024]{1,0:T(4,128)(2,1)S(1)}, u32[]{:S(2)}, u32[]{:S(2)}) %collective-permute-start) | collective-permute-done | bytes 8224 | tf_op jit(solution)/shard_map/ppermute | solution.py:319
  17.2 0.0 copy-done.9
  17.2 38.7 %all_gather.6 = bf16[128,1024]{1,0:T(8,128)(2,1)S(1)} all-gather(bf16[8,1024]{1,0:T(8,128)(2,1)S(1)} %pad_maximum_fusion), channel_id=1, replica_groups={{0,16,32,48,64,80,96,112,128,144,160,176,192,208,224,240},{8,24,40,56,7..., dimensions={0}, use_global_device_ids=true | all-gather | bytes 278528 | tf_op jit(solution)/shard_map/all_gather | solution.py:289
  55.9 7.0 %all_gather.7.tokens = bf16[256,1024]{1,0:T(8,128)(2,1)S(1)} all-gather(bf16[128,1024]{1,0:T(8,128)(2,1)S(1)} %all_gather.6), channel_id=1, replica_groups={{0,8},{16,24},{32,40},{48,56},{64,72},{80,88},{96,104},{112,120},{128,1..., dimensions={0}, use_global_device_ids=true | all-gather | bytes 786432 | tf_op jit(solution)/shard_map/all_gather | solution.py:290
  62.9 0.0 copy-start.1
  63.0 0.0 copy-start.7
  63.0 1.2 hidden.1
  64.1 0.0 copy-start.3
  64.1 0.0 copy-start.4
  64.1 4.4 %all-to-all-start = ((f32[8,16,512]{2,1,0:T(8,128)}), f32[8,16,512]{2,1,0:T(8,128)S(1)}, u32[]{:S(2)}, u32[]{:S(2)}) async-start(f32[8,16,512]{2,1,0:T(8,128)} %bitcast), calls=%async_computation | async-start | bytes 524288 | tf_op jit(solution)/shard_map/all_to_all | solution.py:327
  68.6 0.0 copy-done.1
  68.6 0.0 copy-done.7
  68.6 2.2 %densify.4.after.d3 = bf16[1088,512]{1,0:T(8,128)(2,1)S(1)} custom-call(s32[40]{0:T(128)S(1)} %copy-done.7, bf16[40,4096]{1,0:T(8,128)(2,1)S(1)} %copy-done.1), custom_call_target="tpu_custom_call" | custom-call | tf_op jit(solution)/shard_map/densify/pallas_call | solution.py:199
  70.8 0.0 copy-start.2
  70.8 0.0 copy-start.8
  70.8 5.2 %all-to-all-done.parts = f32[8,16,512]{2,1,0:T(8,128)S(1)} async-done(((f32[8,16,512]{2,1,0:T(8,128)}), f32[8,16,512]{2,1,0:T(8,128)S(1)}, u32[]{:S(2)}, u32[]{:S(2)}) %all-to-all-start) | async-done | bytes 262176 | tf_op jit(solution)/shard_map/all_to_all | solution.py:327
  76.1 0.0 copy-done.3
  76.1 0.0 copy-done.4
  76.1 0.8 gate.2
  76.9 3.5 %all-to-all-start.1 = ((bf16[8,3,16,512]{3,2,1,0:T(8,128)(2,1)}), bf16[8,3,16,512]{3,2,1,0:T(8,128)(2,1)S(1)}, u32[]{:S(2)}, u32[]{:S(2)}) async-start(bf16[8,3,16,512]{3,2,1,0:T(8,128)(2,1)} %gate.2), calls=%async_computation.1 | async-start | bytes 786432 | tf_op jit(solution)/shard_map/all_to_all | solution.py:328
  80.4 0.0 copy-done.2
  80.4 0.0 copy-done.8
  80.4 2.2 %densify.5.d1 = bf16[1088,512]{1,0:T(8,128)(2,1)S(1)} custom-call(s32[40]{0:T(128)S(1)} %copy-done.8, bf16[40,4096]{1,0:T(8,128)(2,1)S(1)} %copy-done.2), custom_call_target="tpu_custom_call" | custom-call | tf_op jit(solution)/shard_map/densify/pallas_call | solution.py:199
  82.6 0.0 copy-start.6
  82.6 6.6 %all-to-all-done.1.acts = bf16[8,3,16,512]{3,2,1,0:T(8,128)(2,1)S(1)} async-done(((bf16[8,3,16,512]{3,2,1,0:T(8,128)(2,1)}), bf16[8,3,16,512]{3,2,1,0:T(8,128)(2,1)S(1)}, u32[]{:S(2)}, u32[]{:S(2)}) %all-to-all-start.1) | async-done | bytes 393248 | tf_op jit(solution)/shard_map/all_to_all | solution.py:328
  89.2 0.8 inputg.1
  90.0 11.0 %all_to_all.20.parts = bf16[4,64,512]{2,1,0:T(8,128)(2,1)S(1)} all-to-all(bf16[4,64,512]{2,1,0:T(8,128)(2,1)S(1)} %bitcast.3), channel_id=1, replica_groups={{0,8,16,24},{32,40,48,56},{64,72,80,88},{96,104,112,120},{128,136,144,1..., dimensions={0} | all-to-all | bytes 524288 | tf_op jit(solution)/shard_map/all_to_all | solution.py:294
  101.0 0.7 near_sum.1
  101.7 12.8 %all-to-all-start.3 = ((bf16[8,8,512]{2,1,0:T(8,128)(2,1)}), bf16[8,8,512]{2,1,0:T(8,128)(2,1)S(1)}, u32[]{:S(2)}, u32[]{:S(2)}) async-start(bf16[8,8,512]{2,1,0:T(8,128)(2,1)} %bitcast.2), calls=%async_computation.3 | async-start | bytes 131072 | tf_op jit(solution)/shard_map/all_to_all | solution.py:294
  114.5 0.0 copy-done.6
  114.5 8.3 %weights.1 = (bf16[40,4096]{1,0:T(8,128)(2,1)}, bf16[40,4096]{1,0:T(8,128)(2,1)}, bf16[40,4096]{1,0:T(8,128)(2,1)}) custom-call(s32[40]{0:T(128)S(1)} %copy-done.8, s32[40]{0:T(128)S(1)} %copy-done.7, s32[40]{0:T(128)S(1)} %copy-done.6, bf16[256,1024]{1,0:T(8,128)(2,1)S(1)} %all_gather.7.tokens, bf16[8,3,16,512]{3,2,1,0:T(8,128)(2,1)S(1)} %all-to-all-done.1.acts), custom_call_target="tpu_custom_call" | custom-call | tf_op jit(solution)/shard_map/weights/pallas_call | solution.py:271
  122.8 15.0 %all-to-all-done.3.parts = bf16[8,8,512]{2,1,0:T(8,128)(2,1)S(1)} async-done(((bf16[8,8,512]{2,1,0:T(8,128)(2,1)}), bf16[8,8,512]{2,1,0:T(8,128)(2,1)S(1)}, u32[]{:S(2)}, u32[]{:S(2)}) %all-to-all-start.3) | async-done | bytes 65568 | tf_op jit(solution)/shard_map/all_to_all | solution.py:294
  137.8 0.6 far_sum.1
  (1 shorter events, 0.0 us)
Async XLA Ops:
  0.6 16.6 %collective-permute-start = (bf16[4,1024]{1,0:T(4,128)(2,1)}, bf16[4,1024]{1,0:T(4,128)(2,1)S(1)}, u32[]{:S(2)}, u32[]{:S(2)}) collective-permute-start(bf16[4,1024]{1,0:T(4,128)(2,1)} %param.10), channel_id=1, source_target_pairs={{0,768},{256,0},{512,256},{768,512},{1,769},{257,1},{513,257},{769... | collective-permute-start | bytes 24584 | tf_op jit(solution)/shard_map/ppermute | solution.py:319
  3.3 1.0 copy-start
  4.3 0.7 copy-start.5
  4.9 12.3 %copy-start.9 = (bf16[4,1024]{1,0:T(4,128)(2,1)S(1)}, bf16[4,1024]{1,0:T(4,128)(2,1)}, u32[]{:S(2)}) copy-start(bf16[4,1024]{1,0:T(4,128)(2,1)} %param.11) | copy-start | bytes 24580
  62.9 5.6 %copy-start.1 = (bf16[40,4096]{1,0:T(8,128)(2,1)S(1)}, bf16[40,4096]{1,0:T(8,128)(2,1)}, u32[]{:S(2)}) copy-start(bf16[40,4096]{1,0:T(8,128)(2,1)} %values.4) | copy-start | bytes 983044
  63.0 5.6 %copy-start.7 = (s32[40]{0:T(128)S(1)}, s32[40]{0:T(128)}, u32[]{:S(2)}) copy-start(s32[40]{0:T(128)} %i3.1) | copy-start | bytes 484
  64.1 11.9 %copy-start.3 = (bf16[16,448]{1,0:T(8,128)(2,1)S(1)}, bf16[16,448]{1,0:T(8,128)(2,1)}, u32[]{:S(2)}) copy-start(bf16[16,448]{1,0:T(8,128)(2,1)} %gate.3) | copy-start | bytes 43012
  64.1 11.9 %copy-start.4 = (bf16[16,448]{1,0:T(8,128)(2,1)S(1)}, bf16[16,448]{1,0:T(8,128)(2,1)}, u32[]{:S(2)}) copy-start(bf16[16,448]{1,0:T(8,128)(2,1)} %up.1) | copy-start | bytes 43012
  64.1 11.9 %all-to-all-start = ((f32[8,16,512]{2,1,0:T(8,128)}), f32[8,16,512]{2,1,0:T(8,128)S(1)}, u32[]{:S(2)}, u32[]{:S(2)}) async-start(f32[8,16,512]{2,1,0:T(8,128)} %bitcast), calls=%async_computation | async-start | bytes 524288 | tf_op jit(solution)/shard_map/all_to_all | solution.py:327
  70.8 9.5 %copy-start.2 = (bf16[40,4096]{1,0:T(8,128)(2,1)S(1)}, bf16[40,4096]{1,0:T(8,128)(2,1)}, u32[]{:S(2)}) copy-start(bf16[40,4096]{1,0:T(8,128)(2,1)} %values.5) | copy-start | bytes 983044
  70.8 9.5 %copy-start.8 = (s32[40]{0:T(128)S(1)}, s32[40]{0:T(128)}, u32[]{:S(2)}) copy-start(s32[40]{0:T(128)} %i1.1) | copy-start | bytes 484
  76.9 12.3 %all-to-all-start.1 = ((bf16[8,3,16,512]{3,2,1,0:T(8,128)(2,1)}), bf16[8,3,16,512]{3,2,1,0:T(8,128)(2,1)S(1)}, u32[]{:S(2)}, u32[]{:S(2)}) async-start(bf16[8,3,16,512]{3,2,1,0:T(8,128)(2,1)} %gate.2), calls=%async_computation.1 | async-start | bytes 786432 | tf_op jit(solution)/shard_map/all_to_all | solution.py:328
  82.6 31.9 %copy-start.6 = (s32[40]{0:T(128)S(1)}, s32[40]{0:T(128)}, u32[]{:S(2)}) copy-start(s32[40]{0:T(128)} %i2.1) | copy-start | bytes 484
  101.7 36.1 %all-to-all-start.3 = ((bf16[8,8,512]{2,1,0:T(8,128)(2,1)}), bf16[8,8,512]{2,1,0:T(8,128)(2,1)S(1)}, u32[]{:S(2)}, u32[]{:S(2)}) async-start(bf16[8,8,512]{2,1,0:T(8,128)(2,1)} %bitcast.2), calls=%async_computation.3 | async-start | bytes 131072 | tf_op jit(solution)/shard_map/all_to_all | solution.py:294

commit v3 on v2

--- a/solution.py
+++ b/solution.py
@@ -109,33 +109,28 @@
     return picked.reshape(picked.shape[0] * picked.shape[1], picked.shape[2])
 
 
-def input_kernel(acts, d1, d3, out):
-    half = out.shape[1]
+def input_kernel(parity, acts, d1, d3, kept, sent):
+    half = kept.shape[1]
     rows = 2 * half
     prod = lax.dot_general(all_rows(acts, 0), d1[:rows], NT, preferred_element_type=F32)
     prod = prod + lax.dot_general(all_rows(acts, 1), d3[:rows], NT, preferred_element_type=F32)
     top = lax.broadcasted_iota(jnp.int32, (8, half), 0) < 4
-    across = out.shape[0] // 32
-
-    def folded(peer):
-        tile = prod[8 * (peer // 2) : 8 * (peer // 2) + 8]
-        left, right = tile[:, :half], tile[:, half:]
-        if peer % 2:
-            return jnp.where(top, pltpu.roll(left, 4, 0), right)
-        return jnp.where(top, left, pltpu.roll(right, 4, 0))
-
-    for q in range(4):
-        for b in range(0, across, 2):
-            base = (q * across + b) * 8
-            both = [folded(4 * b + q), folded(4 * b + 4 + q)]
-            out[base : base + 16, :] = jnp.concatenate(both, 0).astype(BF16)
-
-
-def near_kernel(parts, out):
-    total = parts[0].astype(F32)
-    for i in range(1, parts.shape[0]):
-        total = total + parts[i].astype(F32)
-    out[...] = total.astype(BF16)
+    is_even = parity[0] == 0
+
+    def folded(k):
+        left, right = prod[8 * k : 8 * k + 8, :half], prod[8 * k : 8 * k + 8, half:]
+        even = jnp.where(top, left, pltpu.roll(right, 4, 0))
+        odd = jnp.where(top, pltpu.roll(left, 4, 0), right)
+        return jnp.where(is_even, even, odd), jnp.where(is_even, odd, even)
+
+    for k in range(0, kept.shape[0] // 8, 2):
+        first, second = folded(k), folded(k + 1)
+        kept[8 * k : 8 * k + 16, :] = jnp.concatenate([first[0], second[0]], 0)
+        sent[8 * k : 8 * k + 16, :] = jnp.concatenate([first[1], second[1]], 0).astype(BF16)
+
+
+def near_kernel(kept, got, out):
+    out[...] = (kept[...] + got[...].astype(F32)).astype(BF16)
 
 
 def far_kernel(parts, out):
@@ -147,7 +142,8 @@
     out[:, half:] = pltpu.roll(total, 4, 0)[:4].astype(BF16)
 
 
-def weight_kernel(i1, i3, i2, tokens, acts, o1, o3, o2, spaced, dense, tall, picked, *, rows, cols):
+def weight_kernel(i1, i3, i2, tokens, acts, after, o1, o3, o2, spaced, dense, tall, picked, *, rows, cols):
+    del after
     cap = o1.shape[0]
     count, width = acts.shape[0] * acts.shape[2], acts.shape[3]
     top = lax.broadcasted_iota(jnp.int32, (8, width), 0) < 4
@@ -229,27 +225,27 @@
     )(*near(parts), gate_pre, up_pre, *near(after))
 
 
-def inputg(acts, d1, d3, width):
+def inputg(parity, acts, d1, d3, width):
     tokens = acts.shape[0] * acts.shape[2]
     return pl.pallas_call(
         input_kernel,
-        out_shape=on_chip((2 * tokens, width // 2), BF16),
-        in_specs=[vm()] * 3,
-        out_specs=vm(),
+        out_shape=(on_chip((tokens, width // 2), F32), on_chip((tokens, width // 2), BF16)),
+        in_specs=[sm()] + [vm()] * 3,
+        out_specs=(vm(), vm()),
         compiler_params=pltpu.CompilerParams(vmem_limit_bytes=GRANT),
         name="inputg",
-    )(*near(acts, d1, d3))
-
-
-def near_sum(parts):
+    )(parity, *near(acts, d1, d3))
+
+
+def near_sum(kept, got):
     return pl.pallas_call(
         near_kernel,
-        out_shape=on_chip(parts.shape[1:], BF16),
-        in_specs=[vm()],
+        out_shape=on_chip(got.shape, BF16),
+        in_specs=[vm()] * 2,
         out_specs=vm(),
         compiler_params=pltpu.CompilerParams(vmem_limit_bytes=GRANT),
         name="near_sum",
-    )(*near(parts))
+    )(*near(kept, got))
 
 
 def far_sum(parts):
@@ -263,17 +259,17 @@
     )(*near(parts))
 
 
-def weights(i1, i3, i2, tokens, acts, rows, cols):
+def weights(i1, i3, i2, tokens, acts, after, rows, cols):
     cap = i1.shape[0]
     wide = acts.shape[3]
     count = acts.shape[0] * acts.shape[2]
     o = jax.ShapeDtypeStruct((cap, BLOCK * BLOCK), BF16)
     return pl.pallas_call(
         functools.partial(weight_kernel, rows=rows, cols=cols), out_shape=(o, o, o),
-        in_specs=[sm()] * 3 + [vm()] * 2, out_specs=(vm(),) * 3,
+        in_specs=[sm()] * 3 + [vm()] * 2 + [pl.BlockSpec(memory_space=pl.ANY)], out_specs=(vm(),) * 3,
         scratch_shapes=[pltpu.VMEM((2 * count, wide), F32), pltpu.VMEM((rows * BLOCK + BLOCK, wide), F32),
             pltpu.VMEM((wide, rows * BLOCK), F32), pltpu.VMEM((cap * BLOCK, 128), F32)],
-        compiler_params=pltpu.CompilerParams(vmem_limit_bytes=GRANT), name="weights")(i1, i3, i2, *near(tokens, acts))
+        compiler_params=pltpu.CompilerParams(vmem_limit_bytes=GRANT), name="weights")(i1, i3, i2, *near(tokens, acts), after)
 
 
 def strided(peers, by):
@@ -290,15 +286,13 @@
     return lax.all_gather(skipping, "hid", axis=0, tiled=True, axis_index_groups=adjacent(peers, 2))
 
 
-def exchange(chunks, groups):
-    return lax.all_to_all(chunks, "hid", 0, 0, tiled=True, axis_index_groups=groups)
-
-
-def scatter_sum(total):
+def scatter_sum(kept, sent):
     peers = lax.axis_size("hid")
-    width = total.shape[1]
-    near = near_sum(exchange(total.reshape(4, -1, width), adjacent(peers, 4)))
-    return far_sum(exchange(near.reshape(peers // 4, -1, width), strided(peers, 4)))
+    got = lax.ppermute(sent, "hid", [(peer, peer ^ 1) for peer in range(peers)])
+    total = near_sum(kept, got)
+    parts = total.reshape(peers // 2, -1, total.shape[1])
+    parts = lax.all_to_all(parts, "hid", 0, 0, tiled=True, axis_index_groups=strided(peers, 2))
+    return far_sum(parts), total
 
 
 def body(
@@ -326,8 +320,12 @@
     parts = partial_grad.reshape(peers, partial_grad.shape[0] // peers, partial_grad.shape[1])
     parts = lax.all_to_all(parts, "wid", 0, 0, tiled=True)
     acts = lax.all_to_all(gate(parts, gate_pre, up_pre, third), "wid", 0, 0, tiled=True)
-    input_grad = scatter_sum(inputg(acts, first, third, inputs.shape[1]))
-    w1_grad, w3_grad, w2_grad = weights(w1_index, w3_index, w2_index, tokens, acts, rows, cols)
+    parity = jnp.reshape(lax.axis_index("hid") & 1, (1,)).astype(jnp.int32)
+    kept, sent = inputg(parity, acts, first, third, inputs.shape[1])
+    input_grad, total = scatter_sum(kept, sent)
+    w1_grad, w3_grad, w2_grad = weights(
+        w1_index, w3_index, w2_index, tokens, acts, total, rows, cols
+    )
     return (input_grad, w1_grad, w3_grad, w2_grad)
 
 

time: 140 us -> 139 us (level)
  blocking collectives: 56.7 us -> 45.7 us
  waiting for transfers between devices: 36.8 us -> 43.5 us
  starting transfers between devices: 23.4 us -> 26.4 us
    all_to_all x1 -> x0, blocking collectives: 11 us -> none  [exchange(): lax.all_to_all(chunks, 'hid', 0, 0, tiled=True, axis_index_groups=groups)]
    ppermute x0 -> x1, waiting for transfers between devices: none -> 3.71 us  [scatter_sum(): got = lax.ppermute(sent, 'hid', [(peer, peer ^ 1) for peer in range(peers)])]
    ppermute x0 -> x1, starting transfers between devices: none -> 3.14 us  [scatter_sum(): got = lax.ppermute(sent, 'hid', [(peer, peer ^ 1) for peer in range(peers)])]
    all_to_all x1, waiting for transfers between devices: 15 us -> 17.9 us  [scatter_sum(): lax.all_to_all(parts, 'hid', 0, 0, tiled=True, axis_index_groups=strided(...]
  transfers between devices with their start and end apart: 4 -> 5, of which waited for: 4 -> 5; matrix products, arithmetic and copies ran while one was open for 0% -> 0% of each run, Pallas kernels for 11% -> 11%
where the time goes in v3:
time: 139 us; the launch traced here: 137 us
  blocking collectives  45.7 us (33%)
  waiting for transfers between devices  43.5 us (31%)
  starting transfers between devices  26.4 us (19%)
  Pallas kernels  19.1 us (14%)
  local copies, waits for them, and re-layouts  1.66 us (1%)
    all_gather x1, blocking collectives, gather_tokens(): lax.all_gather(both, 'hid', axis=0, tiled=True, axis_index_groups=strided...  38.7 us
    all_to_all x1, waiting for transfers between devices, scatter_sum(): lax.all_to_all(parts, 'hid', 0, 0, tiled=True, axis_index_groups=strided(...  17.9 us
    all_to_all x1, starting transfers between devices, scatter_sum(): lax.all_to_all(parts, 'hid', 0, 0, tiled=True, axis_index_groups=strided(...  12.7 us
    ppermute x1, waiting for transfers between devices, body(): lax.ppermute(out_grad, 'section', [(i, (i - 1) % sections) for i in range...  10 us
    pallas_call x1, Pallas kernels, weights(): pl.pallas_call(functools.partial(weight_kernel, rows=rows, cols=cols), ou...  8.26 us
    all_gather x1, blocking collectives, gather_tokens(): lax.all_gather(skipping, 'hid', axis=0, tiled=True, axis_index_groups=adj...  7.03 us
    pallas_call x3, Pallas kernels, densify(): pl.pallas_call(functools.partial(dense_kernel, cols=cols), out_shape=on_c...  6.7 us
    all_to_all x1, waiting for transfers between devices, body(): lax.all_to_all(gate(parts, gate_pre, up_pre, third), 'wid', 0, 0, tiled=T...  6.57 us
  transfers between devices with their start and end apart: 5, of which 5 were waited for; matrix products, arithmetic and copies ran while one was open for 0% of the time, Pallas kernels for 11%

profile of v3, /device:TPU:24, one launch (start us, length us, event | category | flops | bytes accessed | tf_op | source)
XLA Modules:
  0.0 137.1 jit_solution(1438852775273181518)
XLA Ops:
  0.6 2.7 %collective-permute-start = (bf16[4,1024]{1,0:T(4,128)(2,1)}, bf16[4,1024]{1,0:T(4,128)(2,1)S(1)}, u32[]{:S(2)}, u32[]{:S(2)}) collective-permute-start(bf16[4,1024]{1,0:T(4,128)(2,1)} %param.10), channel_id=1, source_target_pairs={{0,768},{256,0},{512,256},{768,512},{1,769},{257,1},{513,257},{769... | collective-permute-start | bytes 24584 | tf_op jit(solution)/shard_map/ppermute | solution.py:313
  3.3 0.0 copy-start
  3.3 1.0 copy-done
  4.3 0.0 copy-start.5
  4.3 0.7 copy-done.5
  4.9 0.0 copy-start.9
  4.9 2.2 %densify.3.dense = bf16[512,1024]{1,0:T(8,128)(2,1)S(1)} custom-call(s32[40]{0:T(128)S(1)} %copy-done.5, bf16[40,4096]{1,0:T(8,128)(2,1)S(1)} %copy-done), custom_call_target="tpu_custom_call" | custom-call | tf_op jit(solution)/shard_map/densify/pallas_call | solution.py:195
  7.2 10.0 %collective-permute-done = bf16[4,1024]{1,0:T(4,128)(2,1)S(1)} collective-permute-done((bf16[4,1024]{1,0:T(4,128)(2,1)}, bf16[4,1024]{1,0:T(4,128)(2,1)S(1)}, u32[]{:S(2)}, u32[]{:S(2)}) %collective-permute-start) | collective-permute-done | bytes 8224 | tf_op jit(solution)/shard_map/ppermute | solution.py:313
  17.2 0.0 copy-done.9
  17.2 38.7 %all_gather.6 = bf16[128,1024]{1,0:T(8,128)(2,1)S(1)} all-gather(bf16[8,1024]{1,0:T(8,128)(2,1)S(1)} %pad_maximum_fusion), channel_id=1, replica_groups={{0,16,32,48,64,80,96,112,128,144,160,176,192,208,224,240},{8,24,40,56,7..., dimensions={0}, use_global_device_ids=true | all-gather | bytes 278528 | tf_op jit(solution)/shard_map/all_gather | solution.py:285
  55.9 7.0 %all_gather.7.tokens = bf16[256,1024]{1,0:T(8,128)(2,1)S(1)} all-gather(bf16[128,1024]{1,0:T(8,128)(2,1)S(1)} %all_gather.6), channel_id=1, replica_groups={{0,8},{16,24},{32,40},{48,56},{64,72},{80,88},{96,104},{112,120},{128,1..., dimensions={0}, use_global_device_ids=true | all-gather | bytes 786432 | tf_op jit(solution)/shard_map/all_gather | solution.py:286
  62.9 0.0 copy-start.1
  63.0 0.0 copy-start.7
  63.0 1.2 hidden.1
  64.1 0.0 copy-start.3
  64.1 0.0 copy-start.4
  64.1 4.4 %all-to-all-start = ((f32[8,16,512]{2,1,0:T(8,128)}), f32[8,16,512]{2,1,0:T(8,128)S(1)}, u32[]{:S(2)}, u32[]{:S(2)}) async-start(f32[8,16,512]{2,1,0:T(8,128)} %bitcast.1), calls=%async_computation | async-start | bytes 524288 | tf_op jit(solution)/shard_map/all_to_all | solution.py:321
  68.6 0.0 copy-done.1
  68.6 0.0 copy-done.7
  68.6 2.2 %densify.4.after.d3 = bf16[1088,512]{1,0:T(8,128)(2,1)S(1)} custom-call(s32[40]{0:T(128)S(1)} %copy-done.7, bf16[40,4096]{1,0:T(8,128)(2,1)S(1)} %copy-done.1), custom_call_target="tpu_custom_call" | custom-call | tf_op jit(solution)/shard_map/densify/pallas_call | solution.py:195
  70.8 0.0 copy-start.2
  70.8 0.0 copy-start.8
  70.8 5.2 %all-to-all-done.parts = f32[8,16,512]{2,1,0:T(8,128)S(1)} async-done(((f32[8,16,512]{2,1,0:T(8,128)}), f32[8,16,512]{2,1,0:T(8,128)S(1)}, u32[]{:S(2)}, u32[]{:S(2)}) %all-to-all-start) | async-done | bytes 262176 | tf_op jit(solution)/shard_map/all_to_all | solution.py:321
  76.1 0.0 copy-done.3
  76.1 0.0 copy-done.4
  76.1 0.8 gate.2
  76.9 3.5 %all-to-all-start.1 = ((bf16[8,3,16,512]{3,2,1,0:T(8,128)(2,1)}), bf16[8,3,16,512]{3,2,1,0:T(8,128)(2,1)S(1)}, u32[]{:S(2)}, u32[]{:S(2)}) async-start(bf16[8,3,16,512]{3,2,1,0:T(8,128)(2,1)} %gate.2), calls=%async_computation.1 | async-start | bytes 786432 | tf_op jit(solution)/shard_map/all_to_all | solution.py:322
  80.4 0.0 copy-done.2
  80.4 0.0 copy-done.8
  80.4 2.2 %densify.5.d1 = bf16[1088,512]{1,0:T(8,128)(2,1)S(1)} custom-call(s32[40]{0:T(128)S(1)} %copy-done.8, bf16[40,4096]{1,0:T(8,128)(2,1)S(1)} %copy-done.2), custom_call_target="tpu_custom_call" | custom-call | tf_op jit(solution)/shard_map/densify/pallas_call | solution.py:195
  82.6 6.6 %all-to-all-done.1.acts = bf16[8,3,16,512]{3,2,1,0:T(8,128)(2,1)S(1)} async-done(((bf16[8,3,16,512]{3,2,1,0:T(8,128)(2,1)}), bf16[8,3,16,512]{3,2,1,0:T(8,128)(2,1)S(1)}, u32[]{:S(2)}, u32[]{:S(2)}) %all-to-all-start.1) | async-done | bytes 393248 | tf_op jit(solution)/shard_map/all_to_all | solution.py:322
  89.2 0.0 copy-start.6
  89.2 0.8 inputg.1
  90.0 3.1 %collective-permute-start.1 = (bf16[128,512]{1,0:T(8,128)(2,1)S(1)}, bf16[128,512]{1,0:T(8,128)(2,1)S(1)}, u32[]{:S(2)}, u32[]{:S(2)}) collective-permute-start(bf16[128,512]{1,0:T(8,128)(2,1)S(1)} %get-tuple-element.10), channel_id=1, source_target_pairs={{0,8},{8,0},{16,24},{24,16},{32,40},{40,32},{48,56},{56,48},{64,72... | collective-permute-start | bytes 393224 | tf_op jit(solution)/shard_map/ppermute | solution.py:291
  93.2 3.7 %collective-permute-done.1.got = bf16[128,512]{1,0:T(8,128)(2,1)S(1)} collective-permute-done((bf16[128,512]{1,0:T(8,128)(2,1)S(1)}, bf16[128,512]{1,0:T(8,128)(2,1)S(1)}, u32[]{:S(2)}, u32[]{:S(2)}) %collective-permute-start.1) | collective-permute-done | bytes 131104 | tf_op jit(solution)/shard_map/ppermute | solution.py:291
  96.9 0.7 near_sum.1.after
  97.6 12.7 %all-to-all-start.2 = ((bf16[16,8,512]{2,1,0:T(8,128)(2,1)}), bf16[16,8,512]{2,1,0:T(8,128)(2,1)S(1)}, u32[]{:S(2)}, u32[]{:S(2)}) async-start(bf16[16,8,512]{2,1,0:T(8,128)(2,1)} %bitcast.2), calls=%async_computation.2 | async-start | bytes 262144 | tf_op jit(solution)/shard_map/all_to_all | solution.py:294
  110.3 0.0 copy-done.6
  110.3 8.3 %weights.1 = (bf16[40,4096]{1,0:T(8,128)(2,1)}, bf16[40,4096]{1,0:T(8,128)(2,1)}, bf16[40,4096]{1,0:T(8,128)(2,1)}) custom-call(s32[40]{0:T(128)S(1)} %copy-done.8, s32[40]{0:T(128)S(1)} %copy-done.7, s32[40]{0:T(128)S(1)} %copy-done.6, bf16[256,1024]{1,0:T(8,128)(2,1)S(1)} %all_gather.7.tokens, bf16[8,3,16,512]{3,2,1,0:T(8,128)(2,1)S(1)} %all-to-all-done.1.acts, ...), custom_call_target="tpu_custom_call" | custom-call | tf_op jit(solution)/shard_map/weights/pallas_call | solution.py:267
  118.6 17.9 %all-to-all-done.2.parts = bf16[16,8,512]{2,1,0:T(8,128)(2,1)S(1)} async-done(((bf16[16,8,512]{2,1,0:T(8,128)(2,1)}), bf16[16,8,512]{2,1,0:T(8,128)(2,1)S(1)}, u32[]{:S(2)}, u32[]{:S(2)}) %all-to-all-start.2) | async-done | bytes 131104 | tf_op jit(solution)/shard_map/all_to_all | solution.py:294
  136.5 0.6 far_sum.1
  (1 shorter events, 0.0 us)
Async XLA Ops:
  0.6 16.6 %collective-permute-start = (bf16[4,1024]{1,0:T(4,128)(2,1)}, bf16[4,1024]{1,0:T(4,128)(2,1)S(1)}, u32[]{:S(2)}, u32[]{:S(2)}) collective-permute-start(bf16[4,1024]{1,0:T(4,128)(2,1)} %param.10), channel_id=1, source_target_pairs={{0,768},{256,0},{512,256},{768,512},{1,769},{257,1},{513,257},{769... | collective-permute-start | bytes 24584 | tf_op jit(solution)/shard_map/ppermute | solution.py:313
  3.3 1.0 copy-start
  4.3 0.7 copy-start.5
  4.9 12.3 %copy-start.9 = (bf16[4,1024]{1,0:T(4,128)(2,1)S(1)}, bf16[4,1024]{1,0:T(4,128)(2,1)}, u32[]{:S(2)}) copy-start(bf16[4,1024]{1,0:T(4,128)(2,1)} %param.11) | copy-start | bytes 24580
  62.9 5.6 %copy-start.1 = (bf16[40,4096]{1,0:T(8,128)(2,1)S(1)}, bf16[40,4096]{1,0:T(8,128)(2,1)}, u32[]{:S(2)}) copy-start(bf16[40,4096]{1,0:T(8,128)(2,1)} %values.4) | copy-start | bytes 983044
  63.0 5.6 %copy-start.7 = (s32[40]{0:T(128)S(1)}, s32[40]{0:T(128)}, u32[]{:S(2)}) copy-start(s32[40]{0:T(128)} %i3.1) | copy-start | bytes 484
  64.1 11.9 %copy-start.3 = (bf16[16,448]{1,0:T(8,128)(2,1)S(1)}, bf16[16,448]{1,0:T(8,128)(2,1)}, u32[]{:S(2)}) copy-start(bf16[16,448]{1,0:T(8,128)(2,1)} %gate.3) | copy-start | bytes 43012
  64.1 11.9 %copy-start.4 = (bf16[16,448]{1,0:T(8,128)(2,1)S(1)}, bf16[16,448]{1,0:T(8,128)(2,1)}, u32[]{:S(2)}) copy-start(bf16[16,448]{1,0:T(8,128)(2,1)} %up.1) | copy-start | bytes 43012
  64.1 11.9 %all-to-all-start = ((f32[8,16,512]{2,1,0:T(8,128)}), f32[8,16,512]{2,1,0:T(8,128)S(1)}, u32[]{:S(2)}, u32[]{:S(2)}) async-start(f32[8,16,512]{2,1,0:T(8,128)} %bitcast.1), calls=%async_computation | async-start | bytes 524288 | tf_op jit(solution)/shard_map/all_to_all | solution.py:321
  70.8 9.5 %copy-start.2 = (bf16[40,4096]{1,0:T(8,128)(2,1)S(1)}, bf16[40,4096]{1,0:T(8,128)(2,1)}, u32[]{:S(2)}) copy-start(bf16[40,4096]{1,0:T(8,128)(2,1)} %values.5) | copy-start | bytes 983044
  70.8 9.5 %copy-start.8 = (s32[40]{0:T(128)S(1)}, s32[40]{0:T(128)}, u32[]{:S(2)}) copy-start(s32[40]{0:T(128)} %i1.1) | copy-start | bytes 484
  76.9 12.3 %all-to-all-start.1 = ((bf16[8,3,16,512]{3,2,1,0:T(8,128)(2,1)}), bf16[8,3,16,512]{3,2,1,0:T(8,128)(2,1)S(1)}, u32[]{:S(2)}, u32[]{:S(2)}) async-start(bf16[8,3,16,512]{3,2,1,0:T(8,128)(2,1)} %gate.2), calls=%async_computation.1 | async-start | bytes 786432 | tf_op jit(solution)/shard_map/all_to_all | solution.py:322
  89.2 21.1 %copy-start.6 = (s32[40]{0:T(128)S(1)}, s32[40]{0:T(128)}, u32[]{:S(2)}) copy-start(s32[40]{0:T(128)} %i2.1) | copy-start | bytes 484
  90.0 6.9 %collective-permute-start.1 = (bf16[128,512]{1,0:T(8,128)(2,1)S(1)}, bf16[128,512]{1,0:T(8,128)(2,1)S(1)}, u32[]{:S(2)}, u32[]{:S(2)}) collective-permute-start(bf16[128,512]{1,0:T(8,128)(2,1)S(1)} %get-tuple-element.10), channel_id=1, source_target_pairs={{0,8},{8,0},{16,24},{24,16},{32,40},{40,32},{48,56},{56,48},{64,72... | collective-permute-start | bytes 393224 | tf_op jit(solution)/shard_map/ppermute | solution.py:291
  97.6 39.0 %all-to-all-start.2 = ((bf16[16,8,512]{2,1,0:T(8,128)(2,1)}), bf16[16,8,512]{2,1,0:T(8,128)(2,1)S(1)}, u32[]{:S(2)}, u32[]{:S(2)}) async-start(bf16[16,8,512]{2,1,0:T(8,128)(2,1)} %bitcast.2), calls=%async_computation.2 | async-start | bytes 262144 | tf_op jit(solution)/shard_map/all_to_all | solution.py:294

commit v4 on v3

--- a/solution.py
+++ b/solution.py
@@ -181,6 +181,10 @@
     return tuple(pltpu.with_memory_space_constraint(a, pltpu.VMEM) for a in arrays)
 
 
+def far_off(array):
+    return pltpu.with_memory_space_constraint(array, pltpu.HBM)
+
+
 def on_chip(shape, dtype):
     return pltpu.VMEM(shape, dtype)
 
@@ -312,7 +316,7 @@
     sections = lax.axis_size("section")
     arrived = lax.ppermute(out_grad, "section", [(i, (i - 1) % sections) for i in range(sections)])
     tokens = gather_tokens(jnp.concatenate([arrived, inputs], axis=0))
-    second = densify(w2_index, w2_values, cols, rows)
+    second = densify(far_off(w2_index), far_off(w2_values), cols, rows)
     first = densify(w1_index, w1_values, rows, cols)
     third = densify(w3_index, w3_values, rows, cols)
     partial_grad = hidden(tokens, second)

time: 139 us -> 138 us (level)
  local copies, waits for them, and re-layouts: 1.66 us -> 0.04 us
    unnamed x20 -> x16, local copies, waits for them, and re-layouts: 1.66 us -> 0.04 us
where the time goes in v4:
time: 138 us; the launch traced here: 137 us
  blocking collectives  46.1 us (33%)
  waiting for transfers between devices  44.8 us (32%)
  starting transfers between devices  26.1 us (19%)
  Pallas kernels  19.5 us (14%)
    all_gather x1, blocking collectives, gather_tokens(): lax.all_gather(both, 'hid', axis=0, tiled=True, axis_index_groups=strided...  39.1 us
    all_to_all x1, waiting for transfers between devices, scatter_sum(): lax.all_to_all(parts, 'hid', 0, 0, tiled=True, axis_index_groups=strided(...  18 us
    all_to_all x1, starting transfers between devices, scatter_sum(): lax.all_to_all(parts, 'hid', 0, 0, tiled=True, axis_index_groups=strided(...  12.6 us
    ppermute x1, waiting for transfers between devices, body(): lax.ppermute(out_grad, 'section', [(i, (i - 1) % sections) for i in range...  11.2 us
    pallas_call x1, Pallas kernels, weights(): pl.pallas_call(functools.partial(weight_kernel, rows=rows, cols=cols), ou...  8.26 us
    pallas_call x3, Pallas kernels, densify(): pl.pallas_call(functools.partial(dense_kernel, cols=cols), out_shape=on_c...  7.14 us
    all_gather x1, blocking collectives, gather_tokens(): lax.all_gather(skipping, 'hid', axis=0, tiled=True, axis_index_groups=adj...  7.03 us
    all_to_all x1, waiting for transfers between devices, body(): lax.all_to_all(gate(parts, gate_pre, up_pre, third), 'wid', 0, 0, tiled=T...  6.57 us
  transfers between devices with their start and end apart: 5, of which 5 were waited for; matrix products, arithmetic and copies ran while one was open for 0% of the time, Pallas kernels for 11%

profile of v4, /device:TPU:24, one launch (start us, length us, event | category | flops | bytes accessed | tf_op | source)
XLA Modules:
  0.0 137.4 jit_solution(3978318828021386749)
XLA Ops:
  0.6 0.0 copy-start.7
  0.6 2.7 %collective-permute-start = (bf16[4,1024]{1,0:T(4,128)(2,1)}, bf16[4,1024]{1,0:T(4,128)(2,1)S(1)}, u32[]{:S(2)}, u32[]{:S(2)}) collective-permute-start(bf16[4,1024]{1,0:T(4,128)(2,1)} %param.10), channel_id=1, source_target_pairs={{0,768},{256,0},{512,256},{768,512},{1,769},{257,1},{513,257},{769... | collective-permute-start | bytes 24584 | tf_op jit(solution)/shard_map/ppermute | solution.py:317
  3.3 2.7 %densify.3.dense = bf16[512,1024]{1,0:T(8,128)(2,1)S(1)} custom-call(s32[40]{0:T(128)} %i2.1, bf16[40,4096]{1,0:T(8,128)(2,1)} %values.3), custom_call_target="tpu_custom_call" | custom-call | tf_op jit(solution)/shard_map/densify/pallas_call | solution.py:199
  6.0 11.2 %collective-permute-done = bf16[4,1024]{1,0:T(4,128)(2,1)S(1)} collective-permute-done((bf16[4,1024]{1,0:T(4,128)(2,1)}, bf16[4,1024]{1,0:T(4,128)(2,1)S(1)}, u32[]{:S(2)}, u32[]{:S(2)}) %collective-permute-start) | collective-permute-done | bytes 8224 | tf_op jit(solution)/shard_map/ppermute | solution.py:317
  17.2 0.0 copy-done.7
  17.2 39.1 %all_gather.6 = bf16[128,1024]{1,0:T(8,128)(2,1)S(1)} all-gather(bf16[8,1024]{1,0:T(8,128)(2,1)S(1)} %pad_maximum_fusion), channel_id=1, replica_groups={{0,16,32,48,64,80,96,112,128,144,160,176,192,208,224,240},{8,24,40,56,7..., dimensions={0}, use_global_device_ids=true | all-gather | bytes 278528 | tf_op jit(solution)/shard_map/all_gather | solution.py:289
  56.3 7.0 %all_gather.7.tokens = bf16[256,1024]{1,0:T(8,128)(2,1)S(1)} all-gather(bf16[128,1024]{1,0:T(8,128)(2,1)S(1)} %all_gather.6), channel_id=1, replica_groups={{0,8},{16,24},{32,40},{48,56},{64,72},{80,88},{96,104},{112,120},{128,1..., dimensions={0}, use_global_device_ids=true | all-gather | bytes 786432 | tf_op jit(solution)/shard_map/all_gather | solution.py:290
  63.4 0.0 copy-start
  63.4 0.0 copy-start.5
  63.4 1.2 hidden.1
  64.5 0.0 copy-start.2
  64.5 0.0 copy-start.3
  64.5 4.4 %all-to-all-start = ((f32[8,16,512]{2,1,0:T(8,128)}), f32[8,16,512]{2,1,0:T(8,128)S(1)}, u32[]{:S(2)}, u32[]{:S(2)}) async-start(f32[8,16,512]{2,1,0:T(8,128)} %bitcast.1), calls=%async_computation | async-start | bytes 524288 | tf_op jit(solution)/shard_map/all_to_all | solution.py:325
  69.0 0.0 copy-done
  69.0 0.0 copy-done.5
  69.0 2.2 %densify.4.after.d3 = bf16[1088,512]{1,0:T(8,128)(2,1)S(1)} custom-call(s32[40]{0:T(128)S(1)} %copy-done.5, bf16[40,4096]{1,0:T(8,128)(2,1)S(1)} %copy-done), custom_call_target="tpu_custom_call" | custom-call | tf_op jit(solution)/shard_map/densify/pallas_call | solution.py:199
  71.2 0.0 copy-start.1
  71.2 0.0 copy-start.6
  71.2 5.2 %all-to-all-done.parts = f32[8,16,512]{2,1,0:T(8,128)S(1)} async-done(((f32[8,16,512]{2,1,0:T(8,128)}), f32[8,16,512]{2,1,0:T(8,128)S(1)}, u32[]{:S(2)}, u32[]{:S(2)}) %all-to-all-start) | async-done | bytes 262176 | tf_op jit(solution)/shard_map/all_to_all | solution.py:325
  76.5 0.0 copy-done.2
  76.5 0.0 copy-done.3
  76.5 0.8 gate.2
  77.3 3.5 %all-to-all-start.1 = ((bf16[8,3,16,512]{3,2,1,0:T(8,128)(2,1)}), bf16[8,3,16,512]{3,2,1,0:T(8,128)(2,1)S(1)}, u32[]{:S(2)}, u32[]{:S(2)}) async-start(bf16[8,3,16,512]{3,2,1,0:T(8,128)(2,1)} %gate.2), calls=%async_computation.1 | async-start | bytes 786432 | tf_op jit(solution)/shard_map/all_to_all | solution.py:326
  80.8 0.0 copy-done.1
  80.8 0.0 copy-done.6
  80.8 2.2 %densify.5.d1 = bf16[1088,512]{1,0:T(8,128)(2,1)S(1)} custom-call(s32[40]{0:T(128)S(1)} %copy-done.6, bf16[40,4096]{1,0:T(8,128)(2,1)S(1)} %copy-done.1), custom_call_target="tpu_custom_call" | custom-call | tf_op jit(solution)/shard_map/densify/pallas_call | solution.py:199
  83.0 6.6 %all-to-all-done.1.acts = bf16[8,3,16,512]{3,2,1,0:T(8,128)(2,1)S(1)} async-done(((bf16[8,3,16,512]{3,2,1,0:T(8,128)(2,1)}), bf16[8,3,16,512]{3,2,1,0:T(8,128)(2,1)S(1)}, u32[]{:S(2)}, u32[]{:S(2)}) %all-to-all-start.1) | async-done | bytes 393248 | tf_op jit(solution)/shard_map/all_to_all | solution.py:326
  89.6 0.0 copy-start.4
  89.6 0.8 inputg.1
  90.4 3.0 %collective-permute-start.1 = (bf16[128,512]{1,0:T(8,128)(2,1)S(1)}, bf16[128,512]{1,0:T(8,128)(2,1)S(1)}, u32[]{:S(2)}, u32[]{:S(2)}) collective-permute-start(bf16[128,512]{1,0:T(8,128)(2,1)S(1)} %get-tuple-element.10), channel_id=1, source_target_pairs={{0,8},{8,0},{16,24},{24,16},{32,40},{40,32},{48,56},{56,48},{64,72... | collective-permute-start | bytes 393224 | tf_op jit(solution)/shard_map/ppermute | solution.py:295
  93.5 3.8 %collective-permute-done.1.got = bf16[128,512]{1,0:T(8,128)(2,1)S(1)} collective-permute-done((bf16[128,512]{1,0:T(8,128)(2,1)S(1)}, bf16[128,512]{1,0:T(8,128)(2,1)S(1)}, u32[]{:S(2)}, u32[]{:S(2)}) %collective-permute-start.1) | collective-permute-done | bytes 131104 | tf_op jit(solution)/shard_map/ppermute | solution.py:295
  97.3 0.7 near_sum.1.after
  98.0 12.6 %all-to-all-start.2 = ((bf16[16,8,512]{2,1,0:T(8,128)(2,1)}), bf16[16,8,512]{2,1,0:T(8,128)(2,1)S(1)}, u32[]{:S(2)}, u32[]{:S(2)}) async-start(bf16[16,8,512]{2,1,0:T(8,128)(2,1)} %bitcast.2), calls=%async_computation.2 | async-start | bytes 262144 | tf_op jit(solution)/shard_map/all_to_all | solution.py:298
  110.5 0.0 copy-done.4
  110.6 8.3 %weights.1 = (bf16[40,4096]{1,0:T(8,128)(2,1)}, bf16[40,4096]{1,0:T(8,128)(2,1)}, bf16[40,4096]{1,0:T(8,128)(2,1)}) custom-call(s32[40]{0:T(128)S(1)} %copy-done.6, s32[40]{0:T(128)S(1)} %copy-done.5, s32[40]{0:T(128)S(1)} %copy-done.4, bf16[256,1024]{1,0:T(8,128)(2,1)S(1)} %all_gather.7.tokens, bf16[8,3,16,512]{3,2,1,0:T(8,128)(2,1)S(1)} %all-to-all-done.1.acts, ...), custom_call_target="tpu_custom_call" | custom-call | tf_op jit(solution)/shard_map/weights/pallas_call | solution.py:271
  118.8 18.0 %all-to-all-done.2.parts = bf16[16,8,512]{2,1,0:T(8,128)(2,1)S(1)} async-done(((bf16[16,8,512]{2,1,0:T(8,128)(2,1)}), bf16[16,8,512]{2,1,0:T(8,128)(2,1)S(1)}, u32[]{:S(2)}, u32[]{:S(2)}) %all-to-all-start.2) | async-done | bytes 131104 | tf_op jit(solution)/shard_map/all_to_all | solution.py:298
  136.8 0.6 far_sum.1
  (1 shorter events, 0.0 us)
Async XLA Ops:
  0.6 16.6 %copy-start.7 = (bf16[4,1024]{1,0:T(4,128)(2,1)S(1)}, bf16[4,1024]{1,0:T(4,128)(2,1)}, u32[]{:S(2)}) copy-start(bf16[4,1024]{1,0:T(4,128)(2,1)} %param.11) | copy-start | bytes 24580
  0.6 16.6 %collective-permute-start = (bf16[4,1024]{1,0:T(4,128)(2,1)}, bf16[4,1024]{1,0:T(4,128)(2,1)S(1)}, u32[]{:S(2)}, u32[]{:S(2)}) collective-permute-start(bf16[4,1024]{1,0:T(4,128)(2,1)} %param.10), channel_id=1, source_target_pairs={{0,768},{256,0},{512,256},{768,512},{1,769},{257,1},{513,257},{769... | collective-permute-start | bytes 24584 | tf_op jit(solution)/shard_map/ppermute | solution.py:317
  63.4 5.6 %copy-start = (bf16[40,4096]{1,0:T(8,128)(2,1)S(1)}, bf16[40,4096]{1,0:T(8,128)(2,1)}, u32[]{:S(2)}) copy-start(bf16[40,4096]{1,0:T(8,128)(2,1)} %values.4) | copy-start | bytes 983044
  63.4 5.6 %copy-start.5 = (s32[40]{0:T(128)S(1)}, s32[40]{0:T(128)}, u32[]{:S(2)}) copy-start(s32[40]{0:T(128)} %i3.1) | copy-start | bytes 484
  64.5 11.9 %copy-start.2 = (bf16[16,448]{1,0:T(8,128)(2,1)S(1)}, bf16[16,448]{1,0:T(8,128)(2,1)}, u32[]{:S(2)}) copy-start(bf16[16,448]{1,0:T(8,128)(2,1)} %gate.3) | copy-start | bytes 43012
  64.5 11.9 %copy-start.3 = (bf16[16,448]{1,0:T(8,128)(2,1)S(1)}, bf16[16,448]{1,0:T(8,128)(2,1)}, u32[]{:S(2)}) copy-start(bf16[16,448]{1,0:T(8,128)(2,1)} %up.1) | copy-start | bytes 43012
  64.5 11.9 %all-to-all-start = ((f32[8,16,512]{2,1,0:T(8,128)}), f32[8,16,512]{2,1,0:T(8,128)S(1)}, u32[]{:S(2)}, u32[]{:S(2)}) async-start(f32[8,16,512]{2,1,0:T(8,128)} %bitcast.1), calls=%async_computation | async-start | bytes 524288 | tf_op jit(solution)/shard_map/all_to_all | solution.py:325
  71.2 9.5 %copy-start.1 = (bf16[40,4096]{1,0:T(8,128)(2,1)S(1)}, bf16[40,4096]{1,0:T(8,128)(2,1)}, u32[]{:S(2)}) copy-start(bf16[40,4096]{1,0:T(8,128)(2,1)} %values.5) | copy-start | bytes 983044
  71.2 9.5 %copy-start.6 = (s32[40]{0:T(128)S(1)}, s32[40]{0:T(128)}, u32[]{:S(2)}) copy-start(s32[40]{0:T(128)} %i1.1) | copy-start | bytes 484
  77.3 12.3 %all-to-all-start.1 = ((bf16[8,3,16,512]{3,2,1,0:T(8,128)(2,1)}), bf16[8,3,16,512]{3,2,1,0:T(8,128)(2,1)S(1)}, u32[]{:S(2)}, u32[]{:S(2)}) async-start(bf16[8,3,16,512]{3,2,1,0:T(8,128)(2,1)} %gate.2), calls=%async_computation.1 | async-start | bytes 786432 | tf_op jit(solution)/shard_map/all_to_all | solution.py:326
  89.6 20.9 %copy-start.4 = (s32[40]{0:T(128)S(1)}, s32[40]{0:T(128)}, u32[]{:S(2)}) copy-start(s32[40]{0:T(128)} %i2.1) | copy-start | bytes 484
  90.4 6.9 %collective-permute-start.1 = (bf16[128,512]{1,0:T(8,128)(2,1)S(1)}, bf16[128,512]{1,0:T(8,128)(2,1)S(1)}, u32[]{:S(2)}, u32[]{:S(2)}) collective-permute-start(bf16[128,512]{1,0:T(8,128)(2,1)S(1)} %get-tuple-element.10), channel_id=1, source_target_pairs={{0,8},{8,0},{16,24},{24,16},{32,40},{40,32},{48,56},{56,48},{64,72... | collective-permute-start | bytes 393224 | tf_op jit(solution)/shard_map/ppermute | solution.py:295
  98.0 38.8 %all-to-all-start.2 = ((bf16[16,8,512]{2,1,0:T(8,128)(2,1)}), bf16[16,8,512]{2,1,0:T(8,128)(2,1)S(1)}, u32[]{:S(2)}, u32[]{:S(2)}) async-start(bf16[16,8,512]{2,1,0:T(8,128)(2,1)} %bitcast.2), calls=%async_computation.2 | async-start | bytes 262144 | tf_op jit(solution)/shard_map/all_to_all | solution.py:298
